TPU v7x, 128 devices: a whole 4x4x4 slice. The times are simulated.
128 devices in a mesh: gx: 16 (over z, y), gy: 8 (over x, core).
Axes of the slice: x: 4, y: 4, z: 4, core: 2. Of those that a mesh axis runs over, the one named last changes fastest.
Arguments:
- voxel_xyz: float32 [32768, 3, 128], P(('gx', 'gy')), may hold values from 0 to 1
- voxel_mass: float32 [32768, 128], P(('gx', 'gy')), may hold values from 1 to 64
- candidates: int32 [32768, 8], P(('gx', 'gy')), may hold values from 0 to 65535, as said below
- offload_plan: int32 [32768], P(('gx', 'gy')), may hold values from -1 to 16383, as said below
- seed_xyz: float32 [65536, 3, 128], P(('gx', 'gy')), may hold values from 0 to 1
- seed_pot: float32 [65536, 128], P(('gx', 'gy')), may hold values from -5 to 225
- seed_target: float32 [65536, 128], P(('gx', 'gy')), may hold values from 0.5 to 8
- seed_home: int32 [65536], replicated, may hold values from 0 to 65535, as said below
Outputs:
- dual_pot: float32 [16384, 128], P(('gx', 'gy'))
- seed_moments: float32 [65536, 4, 128], P(('gx', 'gy'))
- new_pot: float32 [65536, 128], P(('gx', 'gy'))
Inputs may be any that keep to these rules, and one draw needn't show every extreme that they name: `candidates`: the 8 ids of one voxel block are distinct seed blocks whose stored rows lie on the block's own device or on the devices one step lower or higher along gx (wrapping), with the same gy index. `offload_plan`: -1 marks a slot with no voxels. Otherwise the value is the row of dual_pot that the block fills; that row lies on a device with the same gx index, and every row is filled by exactly one block. The occupied slots of one device go to the rows of any one device in groups of exactly 32 blocks or not at all. `seed_home`: A permutation of the stored rows.
All inputs are finite; a program needn't handle non-finite values.
Results may differ from a plain program's by a relative error of at most 0.0003.
Values sent between devices are 32-bit elements; how exact they have to be, the bound alone decides.
A program may use at most 64 MiB of HBM per device.

v0:
```python
import math

import jax
import jax.numpy as jnp
from jax import lax
from jax.experimental import pallas as pl
from jax.experimental.pallas import tpu as pltpu
from jax.sharding import PartitionSpec as P

BS = 128
KC = 8
PAIR_CAP = 32
VB = 256
SB = 512
POOL = 3 * SB
N_GX = 16
N_GY = 8
ROWS = 128

EPS = 0.05
STEP = 0.5
LOG2E = math.log2(math.e)
LN2 = math.log(2.0)


def prep_kernel(cand, plan, home, pidx, order, pos, send_row, count):
    me = lax.axis_index("gx")

    @pl.loop(0, VB)
    def _(i):
        send_row[i] = -1

    def slot(v, carry):
        n, ranks = carry
        p = plan[v]

        def occupied(n, *ranks):
            dest = (p // ROWS) % N_GY
            rank = ranks[0]
            for g in range(1, N_GY):
                rank = jnp.where(dest == g, ranks[g], rank)
            order[n] = v
            at = dest * PAIR_CAP + rank
            pos[n] = at
            send_row[at] = p % ROWS
            for k in range(KC):
                s = home[cand[v * KC + k]]
                near = (s // (SB * N_GY) - me + 1 + N_GX) % N_GX
                pidx[n * KC + k] = near * SB + s % SB
            return (n + 1,) + tuple(
                jnp.where(dest == g, ranks[g] + 1, ranks[g]) for g in range(N_GY)
            )

        out = lax.cond(p >= 0, occupied, lambda n, *r: (n,) + tuple(r), n, *ranks)
        return out[0], tuple(out[1:])

    zero = jnp.int32(0)
    n, _ = lax.fori_loop(0, VB, slot, (zero, (zero,) * N_GY))
    count[0] = n


def prep(cand, plan, home):
    smem = pl.BlockSpec(memory_space=pltpu.SMEM)
    i32 = lambda n: jax.ShapeDtypeStruct((n,), jnp.int32)
    return pl.pallas_call(
        prep_kernel,
        in_specs=[smem] * 3,
        out_specs=[smem] * 5,
        out_shape=[i32(VB * KC), i32(VB), i32(VB), i32(VB), i32(1)],
        name="prep",
    )(cand, plan, home)


def bf(x):
    return x.astype(jnp.bfloat16)


def f32(x):
    return x.astype(jnp.float32)


def work_kernel(pidx, order, pos, count, vox, mass, table, mom, dual, ypool, split, wrow):
    n = count[0]
    sub = lax.broadcasted_iota(jnp.int32, (8, BS), 0)
    low = sub < 4
    mom[...] = jnp.zeros_like(mom)
    dual[...] = jnp.zeros_like(dual)

    @pl.loop(0, POOL // 8)
    def _(g):
        for j in range(8):
            t = table[g * 8 + j]
            a = jnp.concatenate([t, t], axis=0)
            hi = f32(bf(a))
            mid = f32(bf(a - hi))
            first = jnp.where(low, hi, mid)
            second = jnp.where(sub == 3, a - hi - mid, jnp.where(sub == 7, 1.0, first))
            ypool[g * 8 + j] = bf(jnp.concatenate([first, second], axis=0))

    def scores(t, slot):
        s = order[t]
        x = vox[s] - 0.5
        xh = f32(bf(x))
        xl = x - xh
        idx = [pidx[t * KC + k] for k in range(KC)]
        top = table[idx[0], 3:4, :]
        for k in range(1, KC):
            top = jnp.maximum(top, table[idx[k], 3:4, :])
        top = f32(bf(jnp.max(top, axis=1, keepdims=True)))
        top = jnp.broadcast_to(top, (1, BS))
        one = jnp.ones((1, BS), jnp.float32)
        xa = bf(jnp.concatenate([xh, one, xh, one, xl, one, xl, -top], axis=0))
        part = None
        for c in range(KC // 2):
            y = jnp.concatenate([ypool[idx[2 * c]], ypool[idx[2 * c + 1]]], axis=1)
            sc = lax.dot_general(
                xa, y, (((0,), (0,)), ((), ())), preferred_element_type=jnp.float32
            )
            e = jnp.exp2(sc)
            eh = bf(e)
            split[slot, 0:BS, c * 256 : (c + 1) * 256] = eh
            split[slot, BS : 2 * BS, c * 256 : (c + 1) * 256] = bf(e - f32(eh))
            p = e[:, :BS] + e[:, BS:]
            part = p if part is None else part + p
        d = jnp.sum(part.T, axis=0, keepdims=True)
        sq = jnp.sum(x * x, axis=0, keepdims=True)
        dual[pl.ds(pos[t], 1), :] = (1.0 / EPS) * sq - LN2 * (top + jnp.log2(d))
        wrow[pl.ds(slot, 1), :] = mass[pl.ds(s, 1), :] / d

    def moments(t, slot):
        s = order[t]
        w = wrow[pl.ds(slot, 1), :]
        f = jnp.concatenate([w, vox[s] * w], axis=0)
        fh = f32(bf(f))
        f8 = bf(jnp.concatenate([fh, f - fh], axis=0))
        m = jnp.dot(
            jnp.concatenate([f8, f8], axis=1), split[slot], preferred_element_type=jnp.float32
        )
        for k in range(KC):
            i = pidx[t * KC + k]
            mom[i] += m[:, k * BS : (k + 1) * BS]

    @pl.when(n > 0)
    def _():
        scores(0, 0)

        @pl.loop(0, n // 2)
        def _(h):
            t = 2 * h + 1
            moments(t - 1, 0)
            scores(t, 1)
            moments(t, 1)
            scores(jnp.minimum(t + 1, n - 1), 0)


def work(pidx, order, pos, count, vox, mass, table):
    vm = pl.BlockSpec(memory_space=pltpu.VMEM)
    smem = pl.BlockSpec(memory_space=pltpu.SMEM)
    return pl.pallas_call(
        work_kernel,
        in_specs=[smem] * 4 + [vm] * 3,
        out_specs=[vm, vm],
        out_shape=[
            jax.ShapeDtypeStruct((POOL, 8, BS), jnp.float32),
            jax.ShapeDtypeStruct((VB, BS), jnp.float32),
        ],
        scratch_shapes=[
            pltpu.VMEM((POOL, 16, BS), jnp.bfloat16),
            pltpu.VMEM((2, 2 * BS, KC * BS), jnp.bfloat16),
            pltpu.VMEM((8, BS), jnp.float32),
        ],
        compiler_params=pltpu.CompilerParams(vmem_limit_bytes=56 << 20),
        name="work",
    )(pidx, order, pos, count, vox, mass, table)


def shifted(value, steps):
    pairs = [(source, (source + steps) % N_GX) for source in range(N_GX)]
    return lax.ppermute(value, "gx", pairs)


def on_device(
    voxel_xyz, voxel_mass, candidates, offload_plan, seed_xyz, seed_pot, seed_target, seed_home
):
    y = seed_xyz - 0.5
    offset = LOG2E * (seed_pot - (1.0 / EPS) * jnp.sum(y * y, axis=1))
    table = jnp.concatenate([(2.0 * LOG2E / EPS) * y, offset[:, None, :]], axis=1)
    pool = jnp.concatenate([shifted(table, 1), table, shifted(table, -1)], axis=0)
    pidx, order, pos, send_row, count = prep(candidates.reshape(-1), offload_plan, seed_home)
    mom, dual = work(pidx, order, pos, count, voxel_xyz, voxel_mass, pool)
    sums = mom[:, :4] + mom[:, 4:]
    index = send_row.astype(jnp.float32).reshape(N_GY, PAIR_CAP)
    index = jnp.pad(index, ((0, 0), (0, BS - PAIR_CAP)))[:, None, :]
    send = jnp.concatenate([dual.reshape(N_GY, PAIR_CAP, BS), index], axis=1)
    got = lax.all_to_all(send, "gy", split_axis=0, concat_axis=0, tiled=True)
    fill = got[:, PAIR_CAP, :PAIR_CAP].reshape(1, -1)
    hot = (lax.broadcasted_iota(jnp.int32, (ROWS, 1), 0).astype(jnp.float32) == fill).astype(
        jnp.float32
    )
    dual_pot = jnp.dot(
        hot, got[:, :PAIR_CAP].reshape(-1, BS), precision=lax.Precision.HIGHEST
    )
    seed_moments = (
        sums[SB : 2 * SB] + shifted(sums[:SB], -1) + shifted(sums[2 * SB :], 1)
    )
    new_pot = seed_pot + STEP * (seed_target - seed_moments[:, 0, :])
    return (dual_pot, seed_moments, new_pot)


def solution(mesh):
    return jax.shard_map(
        on_device,
        mesh=mesh,
        in_specs=(
            P(("gx", "gy"), None, None),
            P(("gx", "gy"), None),
            P(("gx", "gy"), None),
            P(("gx", "gy")),
            P(("gx", "gy"), None, None),
            P(("gx", "gy"), None),
            P(("gx", "gy"), None),
            P(),
        ),
        out_specs=(P(("gx", "gy"), None), P(("gx", "gy"), None, None), P(("gx", "gy"), None)),
        check_vma=False,
    )
```

profile of v0, /device:TPU:5, one launch (start us, length us, event | category | flops | bytes accessed | tf_op | source)
XLA Modules:
  0.0 219.6 jit_solution(5336597427055734933)
XLA Ops:
  0.6 0.0 copy-start.4
  0.6 2.7 %fusion.1 = (f32[512,3,128]{2,1,0:T(4,128)S(1)}, f32[512,128]{1,0:T(8,128)S(1)}) fusion(f32[512,3,128]{2,0,1:T(8,128)} %param.12), kind=kLoop, calls=%fused_computation.7 | loop fusion | flops 720896 | bytes 1835008 | tf_op jit(solution)/shard_map/mul | solution.py:187
  3.4 1.0 subtract_multiply_fusion
  4.4 1.4 pad_maximum_fusion.1
  5.8 1.3 collective-permute-start
  7.1 4.9 %collective-permute-start.1 = (f32[512,4,128]{2,1,0:T(4,128)}, f32[512,4,128]{2,1,0:T(4,128)S(1)}, u32[]{:S(2)}, u32[]{:S(2)}) collective-permute-start(f32[512,4,128]{2,1,0:T(4,128)} %pad_maximum_fusion.1), channel_id=1, source_target_pairs={{0,120},{8,0},{16,8},{24,16},{32,24},{40,32},{48,40},{56,48},{64,5... | collective-permute-start | bytes 3145736 | tf_op jit(solution)/shard_map/ppermute | solution.py:179
  12.1 0.0 copy-done.4
  12.1 0.1 copy.16
  12.2 0.7 reshape.24.cand
  12.9 2.1 copy.19.vox
  15.0 40.5 %prep.1 = (s32[2048]{0:T(1024)}, s32[256]{0:T(256)}, s32[256]{0:T(256)}, s32[256]{0:T(256)}, s32[1]{0:T(128)}) custom-call(s32[2048]{0:T(1024)} %reshape.24.cand, s32[256]{0:T(256)} %plan.1, s32[65536]{0:T(1024)} %home.1), custom_call_target="tpu_custom_call" | custom-call | tf_op jit(solution)/shard_map/prep/pallas_call | solution.py:65
  55.5 0.0 collective-permute-done
  55.5 0.0 collective-permute-done.1
  55.5 8.8 %pad_maximum_fusion.table = f32[1536,4,128]{2,1,0:T(4,128)} fusion(f32[512,4,128]{2,1,0:T(4,128)S(1)} %collective-permute-done.1, f32[512,1,128]{2,1,0:T(1,128)S(1)} %bitcast.7, f32[512,3,128]{2,1,0:T(4,128)S(1)} %get-tuple-element.19, f32[512,4,128]{2,1,0:T(4,128)S(1)} %collective-permute-done), kind=kLoop, calls=%fused_computation | loop fusion | flops 2359296 | bytes 6291456 | tf_op jit(solution)/shard_map/concatenate | solution.py:188
  64.3 115.5 %work.1 = (f32[1536,8,128]{2,1,0:T(8,128)}, f32[256,128]{1,0:T(8,128)}) custom-call(s32[2048]{0:T(1024)} %get-tuple-element.10.pidx, s32[256]{0:T(256)} %get-tuple-element.11.order, s32[256]{0:T(256)} %get-tuple-element.12.pos, s32[1]{0:T(128)} %get-tuple-element.13.count, f32[256,3,128]{2,1,0:T(4,128)} %copy.19.vox, f32[256,128]{1,0:T(8,128)} %mass.1, ...), custom_call_target="tpu_custom_call" | custom-call | tf_op jit(solution)/shard_map/work/pallas_call | solution.py:159
  179.8 5.2 %slice_add_fusion = f32[1536,4,128]{2,1,0:T(4,128)S(1)} fusion(f32[1536,8,128]{2,1,0:T(8,128)} %get-tuple-element.16), kind=kLoop, calls=%fused_computation.1 | loop fusion | flops 786432 | bytes 9437184 | tf_op jit(solution)/shard_map/add | solution.py:191
  185.0 0.0 copy-start.5
  185.0 0.0 copy-start.3
  185.0 1.5 fusion.6
  186.5 0.0 copy-start.1
  186.5 1.5 collective-permute-start.2
  188.0 0.0 collective-permute-start.3
  188.0 0.0 copy-done.5
  188.0 0.1 reshape.26
  188.1 0.0 copy-done.3
  188.1 0.7 pad_maximum_fusion.2
  188.8 5.9 %all-to-all-start = ((f32[8,33,128]{2,1,0:T(8,128)}), f32[8,33,128]{2,1,0:T(8,128)}, u32[]{:S(2)}, u32[]{:S(2)}) async-start(f32[8,33,128]{2,1,0:T(8,128)} %pad_maximum_fusion.2), calls=%async_computation | async-start | bytes 327680 | tf_op jit(solution)/shard_map/all_to_all | solution.py:195
  194.7 3.4 %all-to-all-done = f32[8,33,128]{2,1,0:T(8,128)} async-done(((f32[8,33,128]{2,1,0:T(8,128)}), f32[8,33,128]{2,1,0:T(8,128)}, u32[]{:S(2)}, u32[]{:S(2)}) %all-to-all-start) | async-done | bytes 135200 | tf_op jit(solution)/shard_map/all_to_all | solution.py:195
  198.0 0.8 slice_reduce_fusion
  198.8 0.1 eq.16
  198.9 0.0 copy-start.2
  198.9 1.0 slice.33
  199.9 0.9 fusion.2
  200.7 10.2 %collective-permute-done.2 = f32[512,4,128]{2,1,0:T(4,128)} collective-permute-done((f32[512,4,128]{2,1,0:T(4,128)}, f32[512,4,128]{2,1,0:T(4,128)}, u32[]{:S(2)}, u32[]{:S(2)}) %collective-permute-start.2) | collective-permute-done | bytes 1048608 | tf_op jit(solution)/shard_map/ppermute | solution.py:179
  210.9 5.7 %collective-permute-done.3 = f32[512,4,128]{2,1,0:T(4,128)} collective-permute-done((f32[512,4,128]{2,1,0:T(4,128)}, f32[512,4,128]{2,1,0:T(4,128)}, u32[]{:S(2)}, u32[]{:S(2)}) %collective-permute-start.3) | collective-permute-done | bytes 1048608 | tf_op jit(solution)/shard_map/ppermute | solution.py:179
  216.6 1.9 fusion
  218.5 0.0 copy-start
  218.5 0.2 slice.37
  218.7 0.0 copy-done.1
  218.7 0.0 copy-done.2
  218.8 0.8 multiply_add_fusion
  219.6 0.0 copy-done
  (3 shorter events, 0.0 us)
Async XLA Ops:
  0.6 11.4 %copy-start.4 = (s32[256,8]{0,1:T(8,128)S(1)}, s32[256,8]{0,1:T(8,128)}, u32[]{:S(2)}) copy-start(s32[256,8]{0,1:T(8,128)} %param.10) | copy-start | bytes 24580
  5.8 49.6 %collective-permute-start = (f32[512,4,128]{2,1,0:T(4,128)}, f32[512,4,128]{2,1,0:T(4,128)S(1)}, u32[]{:S(2)}, u32[]{:S(2)}) collective-permute-start(f32[512,4,128]{2,1,0:T(4,128)} %pad_maximum_fusion.1), channel_id=1, source_target_pairs={{0,8},{8,16},{16,24},{24,32},{32,40},{40,48},{48,56},{56,64},{64,7... | collective-permute-start | bytes 3145736 | tf_op jit(solution)/shard_map/ppermute | solution.py:179
  7.1 48.3 %collective-permute-start.1 = (f32[512,4,128]{2,1,0:T(4,128)}, f32[512,4,128]{2,1,0:T(4,128)S(1)}, u32[]{:S(2)}, u32[]{:S(2)}) collective-permute-start(f32[512,4,128]{2,1,0:T(4,128)} %pad_maximum_fusion.1), channel_id=1, source_target_pairs={{0,120},{8,0},{16,8},{24,16},{32,24},{40,32},{48,40},{56,48},{64,5... | collective-permute-start | bytes 3145736 | tf_op jit(solution)/shard_map/ppermute | solution.py:179
  185.0 3.0 %copy-start.5 = (s32[256]{0:T(256)S(1)}, s32[256]{0:T(256)}, u32[]{:S(2)}) copy-start(s32[256]{0:T(256)} %get-tuple-element.15) | copy-start | bytes 3076
  185.0 3.1 %copy-start.3 = (f32[256,128]{1,0:T(8,128)S(1)}, f32[256,128]{1,0:T(8,128)}, u32[]{:S(2)}) copy-start(f32[256,128]{1,0:T(8,128)} %get-tuple-element.14) | copy-start | bytes 393220
  186.5 32.3 %copy-start.1 = (f32[512,128]{1,0:T(8,128)S(1)}, f32[512,128]{1,0:T(8,128)}, u32[]{:S(2)}) copy-start(f32[512,128]{1,0:T(8,128)} %param.13) | copy-start | bytes 786436
  186.5 24.4 %collective-permute-start.2 = (f32[512,4,128]{2,1,0:T(4,128)}, f32[512,4,128]{2,1,0:T(4,128)}, u32[]{:S(2)}, u32[]{:S(2)}) collective-permute-start(f32[512,4,128]{2,1,0:T(4,128)} %get-tuple-element.17), channel_id=1, source_target_pairs={{0,120},{8,0},{16,8},{24,16},{32,24},{40,32},{48,40},{56,48},{64,5... | collective-permute-start | bytes 3145736 | tf_op jit(solution)/shard_map/ppermute | solution.py:179
  188.0 28.7 %collective-permute-start.3 = (f32[512,4,128]{2,1,0:T(4,128)}, f32[512,4,128]{2,1,0:T(4,128)}, u32[]{:S(2)}, u32[]{:S(2)}) collective-permute-start(f32[512,4,128]{2,1,0:T(4,128)} %get-tuple-element.18), channel_id=1, source_target_pairs={{0,8},{8,16},{16,24},{24,32},{32,40},{40,48},{48,56},{56,64},{64,7... | collective-permute-start | bytes 3145736 | tf_op jit(solution)/shard_map/ppermute | solution.py:179
  188.8 9.3 %all-to-all-start = ((f32[8,33,128]{2,1,0:T(8,128)}), f32[8,33,128]{2,1,0:T(8,128)}, u32[]{:S(2)}, u32[]{:S(2)}) async-start(f32[8,33,128]{2,1,0:T(8,128)} %pad_maximum_fusion.2), calls=%async_computation | async-start | bytes 327680 | tf_op jit(solution)/shard_map/all_to_all | solution.py:195
  198.9 19.9 %copy-start.2 = (f32[512,128]{1,0:T(8,128)S(1)}, f32[512,128]{1,0:T(8,128)}, u32[]{:S(2)}) copy-start(f32[512,128]{1,0:T(8,128)} %param.14) | copy-start | bytes 786436
  218.5 1.1 copy-start
where the time goes:
time: 220 us
  Pallas kernels  156 us (71%)
  other arithmetic  22.6 us (10%)
  waiting for transfers between devices  19.2 us (9%)
  starting transfers between devices  13.6 us (6%)
  local copies, waits for them, and re-layouts  6.46 us (3%)
    pallas_call x1, Pallas kernels, work(): pl.pallas_call(work_kernel, in_specs=[smem] * 4 + [vm] * 3, out_specs=[vm...  116 us
    pallas_call x1, Pallas kernels, prep(): pl.pallas_call(prep_kernel, in_specs=[smem] * 3, out_specs=[smem] * 5, ou...  40.5 us
    ppermute x4, waiting for transfers between devices, shifted(): return lax.ppermute(value, 'gx', pairs)  15.9 us
    concatenate x1, other arithmetic, on_device(): jnp.concatenate([shifted(table, 1), table, shifted(table, -1)], axis=0)  8.8 us
    ppermute x4, starting transfers between devices, shifted(): return lax.ppermute(value, 'gx', pairs)  7.71 us
    all_to_all x1, starting transfers between devices, on_device(): got = lax.all_to_all(send, 'gy', split_axis=0, concat_axis=0, tiled=True)  5.92 us
    add x1, other arithmetic, on_device(): sums = mom[:, :4] + mom[:, 4:]  5.19 us
  transfers between devices with their start and end apart: 5, of which 3 were waited for; matrix products, arithmetic and copies ran while one was open for 3% of the time, Pallas kernels for 18%

commit v1 on v0

v1 whole, which is shorter than its diff:
```python
import math

import jax
import jax.numpy as jnp
from jax import lax
from jax.experimental import pallas as pl
from jax.experimental.pallas import tpu as pltpu
from jax.sharding import PartitionSpec as P

BS = 128
KC = 8
PAIR_CAP = 32
VB = 256
SB = 512
POOL = 3 * SB
N_GX = 16
N_GY = 8
ROWS = 128
SLOTS = 4

EPS = 0.05
STEP = 0.5
LOG2E = math.log2(math.e)
LN2 = math.log(2.0)

VMEM = pl.BlockSpec(memory_space=pltpu.VMEM)
SMEM = pl.BlockSpec(memory_space=pltpu.SMEM)


def bf(x):
    return x.astype(jnp.bfloat16)


def f32(x):
    return x.astype(jnp.float32)


def prep_kernel(cand, plan, home, pidx, order, pos, send_row, count, ranks):
    me = lax.axis_index("gx")
    for g in range(N_GY):
        ranks[g] = 0

    @pl.loop(0, VB // 16)
    def _(i):
        for j in range(16):
            send_row[i * 16 + j] = -1

    def slots(h, n):
        for u in range(2):
            v = 2 * h + u
            p = plan[v]
            occupied = (p >= 0).astype(jnp.int32)
            for k in range(KC):
                s = home[cand[k, v]]
                near = ((s >> 12) - me + 1) & 15
                pidx[n * KC + k] = (near << 9) | (s & 511)
            dest = (p >> 7) & 7
            rank = ranks[dest]
            ranks[dest] = rank + occupied
            at = jnp.where(p >= 0, dest * PAIR_CAP + rank, VB)
            order[n] = v
            pos[n] = at
            send_row[at] = p & 127
            n = n + occupied
        return n

    count[0] = lax.fori_loop(0, VB // 2, slots, jnp.int32(0))


def prep(cand, plan, home):
    i32 = lambda n: jax.ShapeDtypeStruct((n,), jnp.int32)
    return pl.pallas_call(
        prep_kernel,
        in_specs=[SMEM] * 3,
        out_specs=[SMEM] * 5,
        out_shape=[i32(VB * KC + KC), i32(VB + 8), i32(VB + 8), i32(VB + 8), i32(1)],
        scratch_shapes=[pltpu.SMEM((N_GY,), jnp.int32)],
        cost_estimate=pl.CostEstimate(flops=1000000, bytes_accessed=30000000, transcendentals=0),
        name="prep",
    )(cand, plan, home)


BUFFERS = ("split", "xat", "part", "top", "f8")


def work_kernel(
    pidx, order, pos, count, vox, mass, low_in, own_in, high_in,
    low_out, own_out, high_out, dual, mom, ypool, *scratch,
):
    n = count[0]
    size = len(BUFFERS)
    bufs = [dict(zip(BUFFERS, scratch[i * size : (i + 1) * size])) for i in range(SLOTS)]
    sub = lax.broadcasted_iota(jnp.int32, (8, BS), 0)
    low = sub < 4
    dual[...] = jnp.zeros_like(dual)
    for q, table in enumerate((low_in, own_in, high_in)):

        @pl.loop(0, SB // 16)
        def _(g):
            for j in range(16):
                i = g * 16 + j
                t = table[pl.ds(i, 4, stride=SB), :]
                a = jnp.concatenate([t, t], axis=0)
                hi = f32(bf(a))
                mid = f32(bf(a - hi))
                first = jnp.where(low, hi, mid)
                second = jnp.where(sub == 3, a - hi - mid, jnp.where(sub == 7, 1.0, first))
                ypool[q * SB + i] = bf(jnp.concatenate([first, second], axis=0))
                mom[q * SB + i] = jnp.zeros((8, BS), jnp.float32)

    def prepare(t, b):
        s = order[t]
        x = vox[pl.ds(s, 3, stride=VB), :] - 0.5
        xh = f32(bf(x))
        xl = x - xh
        tops = [f32(ypool[pidx[t * KC + k], 0:8, :]) for k in range(KC)]
        while len(tops) > 1:
            tops = [jnp.maximum(a, c) for a, c in zip(tops[::2], tops[1::2])]
        top = jnp.max(tops[0][3:4], axis=1, keepdims=True)
        top = jnp.broadcast_to(top, (1, BS))
        one = jnp.ones((1, BS), jnp.float32)
        xa = jnp.concatenate([xh, one, xh, one, xl, one, xl, -top], axis=0)
        b["xat"][...] = bf(xa.T)
        b["top"][0:1, :] = top

    def weigh(t, b):
        idx = [pidx[t * KC + k] for k in range(KC)]
        xat = b["xat"][...]
        part = None
        for c in range(KC // 2):
            y = jnp.concatenate([ypool[idx[2 * c]], ypool[idx[2 * c + 1]]], axis=1)
            e = jnp.exp2(jnp.dot(xat, y, preferred_element_type=jnp.float32))
            eh = bf(e)
            b["split"][0:BS, c * 256 : (c + 1) * 256] = eh
            b["split"][BS : 2 * BS, c * 256 : (c + 1) * 256] = bf(e - f32(eh))
            p = e[:, :BS] + e[:, BS:]
            part = p if part is None else part + p
        b["part"][...] = part

    def norm(t, b):
        s = order[t]
        d = jnp.sum(b["part"][...].T, axis=0, keepdims=True)
        xr = vox[pl.ds(s, 3, stride=VB), :]
        x = xr - 0.5
        sq = jnp.sum(x * x, axis=0, keepdims=True)
        dual[pl.ds(pos[t], 1), :] = (1.0 / EPS) * sq - LN2 * (b["top"][0:1, :] + jnp.log2(d))
        w = mass[pl.ds(s, 1), :] / d
        f = jnp.concatenate([w, xr * w], axis=0)
        fh = f32(bf(f))
        f8 = bf(jnp.concatenate([fh, f - fh], axis=0))
        b["f8"][...] = jnp.concatenate([f8, f8], axis=1)

    def spread(t, b):
        m = jnp.dot(b["f8"][...], b["split"][...], preferred_element_type=jnp.float32)
        for k in range(KC):
            i = pidx[t * KC + k]
            mom[i] += m[:, k * BS : (k + 1) * BS]

    stages = (prepare, weigh, norm, spread)

    def step(t, slot, valid):
        for lag, stage in enumerate(stages):
            if valid(lag):
                stage(t - lag, bufs[(slot - lag) % SLOTS])

    @pl.when(n > 0)
    def _():
        for t in range(SLOTS):
            step(t, t, lambda lag: lag <= t)

        @pl.loop(0, (n - SLOTS) // SLOTS)
        def _(h):
            for u in range(SLOTS):
                step(SLOTS + SLOTS * h + u, u, lambda lag: True)

        for e in range(len(stages) - 1):
            step(n + e, e, lambda lag: lag > e)

    for q, out in enumerate((low_out, own_out, high_out)):

        @pl.loop(0, SB // 16)
        def _(g):
            for j in range(16):
                m = mom[q * SB + g * 16 + j]
                out[g * 16 + j] = m[0:4] + m[4:8]


def work(pidx, order, pos, count, vox, mass, low, own, high):
    moments = jax.ShapeDtypeStruct((SB, 4, BS), jnp.float32)
    scratch = [
        pltpu.VMEM((POOL, 8, BS), jnp.float32),
        pltpu.VMEM((POOL, 16, BS), jnp.bfloat16),
    ]
    scratch += [
        pltpu.VMEM((2 * BS, KC * BS), jnp.bfloat16),
        pltpu.VMEM((BS, 16), jnp.bfloat16),
        pltpu.VMEM((BS, BS), jnp.float32),
        pltpu.VMEM((8, BS), jnp.float32),
        pltpu.VMEM((8, 2 * BS), jnp.bfloat16),
    ] * SLOTS
    return pl.pallas_call(
        work_kernel,
        in_specs=[SMEM] * 4 + [VMEM] * 5,
        out_specs=[VMEM] * 4,
        out_shape=[moments] * 3 + [jax.ShapeDtypeStruct((VB, BS), jnp.float32)],
        scratch_shapes=scratch,
        compiler_params=pltpu.CompilerParams(vmem_limit_bytes=56 << 20),
        name="work",
    )(pidx, order, pos, count, vox, mass, low, own, high)


def shifted(value, steps):
    pairs = [(source, (source + steps) % N_GX) for source in range(N_GX)]
    return lax.ppermute(value, "gx", pairs)


def on_device(
    voxel_xyz, voxel_mass, candidates, offload_plan, seed_xyz, seed_pot, seed_target, seed_home
):
    y = jnp.transpose(seed_xyz, (1, 0, 2)) - 0.5
    offset = LOG2E * (seed_pot - (1.0 / EPS) * (y[0] * y[0] + y[1] * y[1] + y[2] * y[2]))
    table = jnp.concatenate([(2.0 * LOG2E / EPS) * y, offset[None]], axis=0)
    table = table.reshape(4 * SB, BS)
    vox = jnp.transpose(voxel_xyz, (1, 0, 2)).reshape(3 * VB, BS)
    pidx, order, pos, send_row, count = prep(candidates.T, offload_plan, seed_home)
    low, own, high, dual = work(
        pidx, order, pos, count, vox, voxel_mass, shifted(table, 1), table, shifted(table, -1)
    )
    index = send_row[:VB].astype(jnp.float32).reshape(N_GY, PAIR_CAP)
    index = jnp.pad(index, ((0, 0), (0, BS - PAIR_CAP)))[:, None, :]
    send = jnp.concatenate([dual.reshape(N_GY, PAIR_CAP, BS), index], axis=1)
    got = lax.all_to_all(send, "gy", split_axis=0, concat_axis=0, tiled=True)
    fill = got[:, PAIR_CAP, :PAIR_CAP].reshape(1, -1)
    hot = (lax.broadcasted_iota(jnp.int32, (ROWS, 1), 0).astype(jnp.float32) == fill).astype(
        jnp.float32
    )
    dual_pot = jnp.dot(
        hot, got[:, :PAIR_CAP].reshape(-1, BS), precision=lax.Precision.HIGHEST
    )
    seed_moments = own + shifted(low, -1) + shifted(high, 1)
    new_pot = seed_pot + STEP * (seed_target - seed_moments[:, 0, :])
    return (dual_pot, seed_moments, new_pot)


def solution(mesh):
    return jax.shard_map(
        on_device,
        mesh=mesh,
        in_specs=(
            P(("gx", "gy"), None, None),
            P(("gx", "gy"), None),
            P(("gx", "gy"), None),
            P(("gx", "gy")),
            P(("gx", "gy"), None, None),
            P(("gx", "gy"), None),
            P(("gx", "gy"), None),
            P(),
        ),
        out_specs=(P(("gx", "gy"), None), P(("gx", "gy"), None, None), P(("gx", "gy"), None)),
        check_vma=False,
    )
```

time: 220 us -> 128 us (0.58)
  the two profiles are of different devices: /device:TPU:5 before, /device:TPU:1 now
where the time goes in v1:
time: 128 us; the launch traced here: 126 us
  Pallas kernels  78.4 us (61%)
  waiting for transfers between devices  19 us (15%)
  starting transfers between devices  18.1 us (14%)
  local copies, waits for them, and re-layouts  5.27 us (4%)
  other arithmetic  3.99 us (3%)
    pallas_call x1, Pallas kernels, work(): pl.pallas_call(work_kernel, in_specs=[SMEM] * 4 + [VMEM] * 5, out_specs=[...  63 us
    pallas_call x1, Pallas kernels, prep(): pl.pallas_call(prep_kernel, in_specs=[SMEM] * 3, out_specs=[SMEM] * 5, ou...  15.5 us
    ppermute x4, waiting for transfers between devices, shifted(): return lax.ppermute(value, 'gx', pairs)  13.1 us
    ppermute x4, starting transfers between devices, shifted(): return lax.ppermute(value, 'gx', pairs)  12 us
    all_to_all x1, starting transfers between devices, on_device(): got = lax.all_to_all(send, 'gy', split_axis=0, concat_axis=0, tiled=True)  6.12 us
    all_to_all x1, waiting for transfers between devices, on_device(): got = lax.all_to_all(send, 'gy', split_axis=0, concat_axis=0, tiled=True)  5.87 us
    unnamed x18, local copies, waits for them, and re-layouts  3.23 us
  transfers between devices with their start and end apart: 5, of which 3 were waited for; matrix products, arithmetic and copies ran while one was open for 3% of the time, Pallas kernels for 12%

profile of v1, /device:TPU:1, one launch (start us, length us, event | category | flops | bytes accessed | tf_op | source)
XLA Modules:
  0.0 126.4 jit_solution(15659546025227278628)
XLA Ops:
  0.6 0.0 copy-start.1
  0.6 1.3 add_bitcast_fusion
  1.9 0.1 copy-done.1
  2.0 0.0 copy-start.3
  2.0 0.1 broadcast_multiply_fusion
  2.1 0.9 copy-done.3
  3.0 0.1 fusion.5
  3.0 0.1 pad_maximum_fusion
  3.1 0.0 copy-start
  3.1 2.2 %collective-permute-start = (f32[2048,128]{1,0:T(8,128)S(1)}, f32[2048,128]{1,0:T(8,128)S(1)}, u32[]{:S(2)}, u32[]{:S(2)}) collective-permute-start(f32[2048,128]{1,0:T(8,128)S(1)} %bitcast.28), channel_id=1, source_target_pairs={{0,8},{8,16},{16,24},{24,32},{32,40},{40,48},{48,56},{56,64},{64,7... | collective-permute-start | bytes 3145736 | tf_op jit(solution)/shard_map/ppermute | solution.py:214
  5.3 5.0 %collective-permute-start.1 = (f32[2048,128]{1,0:T(8,128)S(1)}, f32[2048,128]{1,0:T(8,128)S(1)}, u32[]{:S(2)}, u32[]{:S(2)}) collective-permute-start(f32[2048,128]{1,0:T(8,128)S(1)} %bitcast.29), channel_id=1, source_target_pairs={{0,120},{8,0},{16,8},{24,16},{32,24},{40,32},{48,40},{56,48},{64,5... | collective-permute-start | bytes 3145736 | tf_op jit(solution)/shard_map/ppermute | solution.py:214
  10.3 15.5 %prep.1 = (s32[2056]{0:T(1024)}, s32[264]{0:T(512)}, s32[264]{0:T(512)}, s32[264]{0:T(512)}, s32[1]{0:T(128)}) custom-call(s32[8,256]{1,0:T(8,128)} %bitcast.41, s32[256]{0:T(256)} %plan.1, s32[65536]{0:T(1024)} %home.1), custom_call_target="tpu_custom_call" | custom-call | flops 1000000 | bytes 30000000 | tf_op jit(solution)/shard_map/prep/pallas_call | solution.py:72
  25.8 7.3 %collective-permute-done.low_in = f32[2048,128]{1,0:T(8,128)S(1)} collective-permute-done((f32[2048,128]{1,0:T(8,128)S(1)}, f32[2048,128]{1,0:T(8,128)S(1)}, u32[]{:S(2)}, u32[]{:S(2)}) %collective-permute-start) | collective-permute-done | bytes 1048608 | tf_op jit(solution)/shard_map/ppermute | solution.py:214
  33.1 0.0 copy-start.5
  33.1 0.0 collective-permute-done.1.high_in
  33.1 0.0 copy-start.6
  33.1 0.0 copy-done
  33.1 1.0 copy-done.5
  34.1 0.3 copy-done.6
  34.4 0.0 copy-start.8
  34.4 63.0 %work.1 = (f32[512,4,128]{2,1,0:T(4,128)}, f32[512,4,128]{2,1,0:T(4,128)}, f32[512,4,128]{2,1,0:T(4,128)}, f32[256,128]{1,0:T(8,128)}) custom-call(s32[2056]{0:T(1024)} %get-tuple-element.12.pidx, s32[264]{0:T(512)} %get-tuple-element.13.order, s32[264]{0:T(512)} %get-tuple-element.14.pos, s32[1]{0:T(128)} %get-tuple-element.15.count, f32[768,128]{1,0:T(8,128)} %bitcast.38, ...), custom_call_target="tpu_custom_call" | custom-call | tf_op jit(solution)/shard_map/work/pallas_call | solution.py:201
  97.4 0.0 copy-start.4
  97.4 0.0 collective-permute-start.3
  97.4 4.8 %collective-permute-start.2 = (f32[512,4,128]{2,1,0:T(4,128)}, f32[512,4,128]{2,1,0:T(4,128)S(1)}, u32[]{:S(2)}, u32[]{:S(2)}) collective-permute-start(f32[512,4,128]{2,1,0:T(4,128)} %get-tuple-element.19), channel_id=1, source_target_pairs={{0,120},{8,0},{16,8},{24,16},{32,24},{40,32},{48,40},{56,48},{64,5... | collective-permute-start | bytes 3145736 | tf_op jit(solution)/shard_map/ppermute | solution.py:214
  102.2 0.0 copy-done.8
  102.2 0.1 convert_element_type.20
  102.3 1.6 %pad_maximum_fusion.1 = f32[8,33,128]{2,1,0:T(8,128)} fusion(f32[8,1,128]{2,1,0:T(1,128)S(1)} %bitcast.40, f32[8,32,128]{2,1,0:T(8,128)} %bitcast.39), kind=kLoop, calls=%fused_computation.15 | loop fusion | flops 33792 | bytes 270336 | tf_op jit(solution)/shard_map/concatenate | solution.py:231
  103.9 6.1 %all-to-all-start = ((f32[8,33,128]{2,1,0:T(8,128)}), f32[8,33,128]{2,1,0:T(8,128)}, u32[]{:S(2)}, u32[]{:S(2)}) async-start(f32[8,33,128]{2,1,0:T(8,128)} %pad_maximum_fusion.1), calls=%async_computation | async-start | bytes 327680 | tf_op jit(solution)/shard_map/all_to_all | solution.py:232
  110.0 5.9 %all-to-all-done = f32[8,33,128]{2,1,0:T(8,128)} async-done(((f32[8,33,128]{2,1,0:T(8,128)}), f32[8,33,128]{2,1,0:T(8,128)}, u32[]{:S(2)}, u32[]{:S(2)}) %all-to-all-start) | async-done | bytes 135200 | tf_op jit(solution)/shard_map/all_to_all | solution.py:232
  115.9 0.8 slice_reduce_fusion
  116.6 0.1 eq.16
  116.7 0.9 slice.35
  117.6 0.9 fusion.7
  118.5 5.8 %collective-permute-done.3 = f32[512,4,128]{2,1,0:T(4,128)S(1)} collective-permute-done((f32[512,4,128]{2,1,0:T(4,128)}, f32[512,4,128]{2,1,0:T(4,128)S(1)}, u32[]{:S(2)}, u32[]{:S(2)}) %collective-permute-start.3) | collective-permute-done | bytes 1048608 | tf_op jit(solution)/shard_map/ppermute | solution.py:214
  124.3 0.0 collective-permute-done.2
  124.3 0.0 copy-done.4
  124.4 0.2 add_add_fusion
  124.5 0.0 copy-start.2
  124.5 0.0 copy-start.7
  124.5 0.2 slice.36
  124.7 0.9 copy-done.7
  125.7 0.7 multiply_add_fusion
  126.4 0.0 copy-done.2
  (3 shorter events, 0.0 us)
Async XLA Ops:
  0.6 1.4 %copy-start.1 = (f32[512,3,128]{2,0,1:T(8,128)S(1)}, f32[512,3,128]{2,0,1:T(8,128)}, u32[]{:S(2)}) copy-start(f32[512,3,128]{2,0,1:T(8,128)} %param.12) | copy-start | bytes 2359300
  2.0 0.9 copy-start.3
  3.1 30.0 %copy-start = (f32[4,512,128]{2,1,0:T(8,128)}, f32[4,512,128]{2,1,0:T(8,128)S(1)}, u32[]{:S(2)}) copy-start(f32[4,512,128]{2,1,0:T(8,128)S(1)} %pad_maximum_fusion) | copy-start | bytes 3145732
  3.1 30.0 %collective-permute-start = (f32[2048,128]{1,0:T(8,128)S(1)}, f32[2048,128]{1,0:T(8,128)S(1)}, u32[]{:S(2)}, u32[]{:S(2)}) collective-permute-start(f32[2048,128]{1,0:T(8,128)S(1)} %bitcast.28), channel_id=1, source_target_pairs={{0,8},{8,16},{16,24},{24,32},{32,40},{40,48},{48,56},{56,64},{64,7... | collective-permute-start | bytes 3145736 | tf_op jit(solution)/shard_map/ppermute | solution.py:214
  5.3 27.8 %collective-permute-start.1 = (f32[2048,128]{1,0:T(8,128)S(1)}, f32[2048,128]{1,0:T(8,128)S(1)}, u32[]{:S(2)}, u32[]{:S(2)}) collective-permute-start(f32[2048,128]{1,0:T(8,128)S(1)} %bitcast.29), channel_id=1, source_target_pairs={{0,120},{8,0},{16,8},{24,16},{32,24},{40,32},{48,40},{56,48},{64,5... | collective-permute-start | bytes 3145736 | tf_op jit(solution)/shard_map/ppermute | solution.py:214
  33.1 1.0 copy-start.5
  33.1 1.3 %copy-start.6 = (f32[2048,128]{1,0:T(8,128)}, f32[2048,128]{1,0:T(8,128)S(1)}, u32[]{:S(2)}) copy-start(f32[2048,128]{1,0:T(8,128)S(1)} %collective-permute-done.1.high_in) | copy-start | bytes 3145732
  34.4 67.7 %copy-start.8 = (s32[264]{0:T(512)S(1)}, s32[264]{0:T(512)}, u32[]{:S(2)}) copy-start(s32[264]{0:T(512)} %get-tuple-element.17) | copy-start | bytes 3172
  97.4 27.0 %copy-start.4 = (f32[512,4,128]{2,1,0:T(4,128)S(1)}, f32[512,4,128]{2,1,0:T(4,128)}, u32[]{:S(2)}) copy-start(f32[512,4,128]{2,1,0:T(4,128)} %get-tuple-element.18) | copy-start | bytes 3145732
  97.4 26.9 %collective-permute-start.3 = (f32[512,4,128]{2,1,0:T(4,128)}, f32[512,4,128]{2,1,0:T(4,128)S(1)}, u32[]{:S(2)}, u32[]{:S(2)}) collective-permute-start(f32[512,4,128]{2,1,0:T(4,128)} %get-tuple-element.20), channel_id=1, source_target_pairs={{0,8},{8,16},{16,24},{24,32},{32,40},{40,48},{48,56},{56,64},{64,7... | collective-permute-start | bytes 3145736 | tf_op jit(solution)/shard_map/ppermute | solution.py:214
  97.4 26.9 %collective-permute-start.2 = (f32[512,4,128]{2,1,0:T(4,128)}, f32[512,4,128]{2,1,0:T(4,128)S(1)}, u32[]{:S(2)}, u32[]{:S(2)}) collective-permute-start(f32[512,4,128]{2,1,0:T(4,128)} %get-tuple-element.19), channel_id=1, source_target_pairs={{0,120},{8,0},{16,8},{24,16},{32,24},{40,32},{48,40},{56,48},{64,5... | collective-permute-start | bytes 3145736 | tf_op jit(solution)/shard_map/ppermute | solution.py:214
  103.9 12.0 %all-to-all-start = ((f32[8,33,128]{2,1,0:T(8,128)}), f32[8,33,128]{2,1,0:T(8,128)}, u32[]{:S(2)}, u32[]{:S(2)}) async-start(f32[8,33,128]{2,1,0:T(8,128)} %pad_maximum_fusion.1), calls=%async_computation | async-start | bytes 327680 | tf_op jit(solution)/shard_map/all_to_all | solution.py:232
  124.5 1.9 %copy-start.2 = (f32[256,8,128]{2,1,0:T(8,128)}, f32[256,8,128]{2,1,0:T(8,128)S(1)}, u32[]{:S(2)}) copy-start(f32[256,8,128]{2,1,0:T(8,128)S(1)} %add_add_fusion) | copy-start | bytes 3145732
  124.5 1.1 copy-start.7

commit v2 on v1

--- a/solution.py
+++ b/solution.py
@@ -17,6 +17,7 @@
 N_GY = 8
 ROWS = 128
 SLOTS = 4
+TOGETHER = 2
 
 EPS = 0.05
 STEP = 0.5
@@ -89,7 +90,7 @@
 ):
     n = count[0]
     size = len(BUFFERS)
-    bufs = [dict(zip(BUFFERS, scratch[i * size : (i + 1) * size])) for i in range(SLOTS)]
+    bufs = [dict(zip(BUFFERS, scratch[i * size : (i + 1) * size])) for i in range(SLOTS * TOGETHER)]
     sub = lax.broadcasted_iota(jnp.int32, (8, BS), 0)
     low = sub < 4
     dual[...] = jnp.zeros_like(dual)
@@ -123,19 +124,32 @@
         b["xat"][...] = bf(xa.T)
         b["top"][0:1, :] = top
 
-    def weigh(t, b):
-        idx = [pidx[t * KC + k] for k in range(KC)]
-        xat = b["xat"][...]
+    def weigh_and_spread(t, b, told, bold):
         part = None
         for c in range(KC // 2):
-            y = jnp.concatenate([ypool[idx[2 * c]], ypool[idx[2 * c + 1]]], axis=1)
-            e = jnp.exp2(jnp.dot(xat, y, preferred_element_type=jnp.float32))
-            eh = bf(e)
-            b["split"][0:BS, c * 256 : (c + 1) * 256] = eh
-            b["split"][BS : 2 * BS, c * 256 : (c + 1) * 256] = bf(e - f32(eh))
-            p = e[:, :BS] + e[:, BS:]
-            part = p if part is None else part + p
-        b["part"][...] = part
+            if t is not None:
+                y = [ypool[pidx[t * KC + 2 * c + j]] for j in range(2)]
+                sc = jnp.dot(
+                    b["xat"][...],
+                    jnp.concatenate(y, axis=1),
+                    preferred_element_type=jnp.float32,
+                )
+            if told is not None:
+                e2 = jnp.concatenate([bold["split"][2 * c], bold["split"][2 * c + 1]], axis=1)
+                m = jnp.dot(bold["f8"][...], e2, preferred_element_type=jnp.float32)
+                for j in range(2):
+                    mom[pidx[told * KC + 2 * c + j]] += m[:, j * BS : (j + 1) * BS]
+            if t is not None:
+                e = jnp.exp2(sc)
+                eh = bf(e)
+                el = bf(e - f32(eh))
+                for j in range(2):
+                    b["split"][2 * c + j, 0:BS, :] = eh[:, j * BS : (j + 1) * BS]
+                    b["split"][2 * c + j, BS:, :] = el[:, j * BS : (j + 1) * BS]
+                p = e[:, :BS] + e[:, BS:]
+                part = p if part is None else part + p
+        if t is not None:
+            b["part"][...] = part
 
     def norm(t, b):
         s = order[t]
@@ -150,31 +164,32 @@
         f8 = bf(jnp.concatenate([fh, f - fh], axis=0))
         b["f8"][...] = jnp.concatenate([f8, f8], axis=1)
 
-    def spread(t, b):
-        m = jnp.dot(b["f8"][...], b["split"][...], preferred_element_type=jnp.float32)
-        for k in range(KC):
-            i = pidx[t * KC + k]
-            mom[i] += m[:, k * BS : (k + 1) * BS]
-
-    stages = (prepare, weigh, norm, spread)
-
-    def step(t, slot, valid):
-        for lag, stage in enumerate(stages):
-            if valid(lag):
-                stage(t - lag, bufs[(slot - lag) % SLOTS])
+    def step(g, slot, valid):
+        for stage in range(3):
+            for u in range(TOGETHER):
+                at = lambda lag: (g - lag) * TOGETHER + u if valid(lag) else None
+                buf = lambda lag: bufs[((slot - lag) % SLOTS) * TOGETHER + u]
+                if stage == 0 and valid(0):
+                    prepare(at(0), buf(0))
+                if stage == 1 and (valid(1) or valid(3)):
+                    weigh_and_spread(at(1), buf(1), at(3), buf(3))
+                if stage == 2 and valid(2):
+                    norm(at(2), buf(2))
+
+    groups = n // TOGETHER
 
     @pl.when(n > 0)
     def _():
-        for t in range(SLOTS):
-            step(t, t, lambda lag: lag <= t)
-
-        @pl.loop(0, (n - SLOTS) // SLOTS)
+        for g in range(SLOTS):
+            step(g, g, lambda lag: lag <= g)
+
+        @pl.loop(0, (groups - SLOTS) // SLOTS)
         def _(h):
             for u in range(SLOTS):
                 step(SLOTS + SLOTS * h + u, u, lambda lag: True)
 
-        for e in range(len(stages) - 1):
-            step(n + e, e, lambda lag: lag > e)
+        for e in range(3):
+            step(groups + e, e, lambda lag: lag > e)
 
     for q, out in enumerate((low_out, own_out, high_out)):
 
@@ -192,12 +207,12 @@
         pltpu.VMEM((POOL, 16, BS), jnp.bfloat16),
     ]
     scratch += [
-        pltpu.VMEM((2 * BS, KC * BS), jnp.bfloat16),
+        pltpu.VMEM((KC, 2 * BS, BS), jnp.bfloat16),
         pltpu.VMEM((BS, 16), jnp.bfloat16),
         pltpu.VMEM((BS, BS), jnp.float32),
         pltpu.VMEM((8, BS), jnp.float32),
         pltpu.VMEM((8, 2 * BS), jnp.bfloat16),
-    ] * SLOTS
+    ] * (SLOTS * TOGETHER)
     return pl.pallas_call(
         work_kernel,
         in_specs=[SMEM] * 4 + [VMEM] * 5,

time: 128 us -> 114 us (0.89); the launches traced: 126 us -> 114 us
  Pallas kernels: 78.4 us -> 65.2 us
    pallas_call x1, Pallas kernels: 63 us -> 49.7 us  [work(): pl.pallas_call(work_kernel, in_specs=[SMEM] * 4 + [VMEM] * 5, out_specs=[...]
  transfers between devices with their start and end apart: 5 -> 5, of which waited for: 3 -> 3; matrix products, arithmetic and copies ran while one was open for 3% -> 4% of each run, Pallas kernels for 12% -> 14%
where the time goes in v2:
time: 114 us
  Pallas kernels  65.2 us (57%)
  waiting for transfers between devices  19.9 us (17%)
  starting transfers between devices  17.8 us (16%)
  local copies, waits for them, and re-layouts  5.27 us (5%)
  other arithmetic  3.99 us (4%)
    pallas_call x1, Pallas kernels, work(): pl.pallas_call(work_kernel, in_specs=[SMEM] * 4 + [VMEM] * 5, out_specs=[...  49.7 us
    pallas_call x1, Pallas kernels, prep(): pl.pallas_call(prep_kernel, in_specs=[SMEM] * 3, out_specs=[SMEM] * 5, ou...  15.5 us
    ppermute x4, waiting for transfers between devices, shifted(): return lax.ppermute(value, 'gx', pairs)  14 us
    ppermute x4, starting transfers between devices, shifted(): return lax.ppermute(value, 'gx', pairs)  12 us
    all_to_all x1, waiting for transfers between devices, on_device(): got = lax.all_to_all(send, 'gy', split_axis=0, concat_axis=0, tiled=True)  5.87 us
    all_to_all x1, starting transfers between devices, on_device(): got = lax.all_to_all(send, 'gy', split_axis=0, concat_axis=0, tiled=True)  5.83 us
    unnamed x18, local copies, waits for them, and re-layouts  3.23 us
  transfers between devices with their start and end apart: 5, of which 3 were waited for; matrix products, arithmetic and copies ran while one was open for 4% of the time, Pallas kernels for 14%

profile of v2, /device:TPU:1, one launch (start us, length us, event | category | flops | bytes accessed | tf_op | source)
XLA Modules:
  0.0 113.8 jit_solution(13202459821578061777)
XLA Ops:
  0.6 0.0 copy-start.1
  0.6 1.3 %add_bitcast_fusion = f32[3,512,128]{2,1,0:T(8,128)S(1)} fusion(f32[512,3,128]{2,0,1:T(8,128)} %param.12), kind=kLoop, calls=%fused_computation.2 | loop fusion | flops 196608 | bytes 1572864 | tf_op jit(solution)/shard_map/sub | solution.py:235
  1.9 0.1 copy-done.1
  2.0 0.0 copy-start.3
  2.0 0.1 broadcast_multiply_fusion
  2.1 0.9 copy-done.3
  3.0 0.1 fusion.5
  3.0 0.1 pad_maximum_fusion
  3.1 0.0 copy-start
  3.1 2.2 %collective-permute-start = (f32[2048,128]{1,0:T(8,128)S(1)}, f32[2048,128]{1,0:T(8,128)S(1)}, u32[]{:S(2)}, u32[]{:S(2)}) collective-permute-start(f32[2048,128]{1,0:T(8,128)S(1)} %bitcast.28), channel_id=1, source_target_pairs={{0,8},{8,16},{16,24},{24,32},{32,40},{40,48},{48,56},{56,64},{64,7... | collective-permute-start | bytes 3145736 | tf_op jit(solution)/shard_map/ppermute | solution.py:229
  5.3 5.0 %collective-permute-start.1 = (f32[2048,128]{1,0:T(8,128)S(1)}, f32[2048,128]{1,0:T(8,128)S(1)}, u32[]{:S(2)}, u32[]{:S(2)}) collective-permute-start(f32[2048,128]{1,0:T(8,128)S(1)} %bitcast.29), channel_id=1, source_target_pairs={{0,120},{8,0},{16,8},{24,16},{32,24},{40,32},{48,40},{56,48},{64,5... | collective-permute-start | bytes 3145736 | tf_op jit(solution)/shard_map/ppermute | solution.py:229
  10.3 15.5 %prep.1 = (s32[2056]{0:T(1024)}, s32[264]{0:T(512)}, s32[264]{0:T(512)}, s32[264]{0:T(512)}, s32[1]{0:T(128)}) custom-call(s32[8,256]{1,0:T(8,128)} %bitcast.41, s32[256]{0:T(256)} %plan.1, s32[65536]{0:T(1024)} %home.1), custom_call_target="tpu_custom_call" | custom-call | flops 1000000 | bytes 30000000 | tf_op jit(solution)/shard_map/prep/pallas_call | solution.py:73
  25.8 7.3 %collective-permute-done.low_in = f32[2048,128]{1,0:T(8,128)S(1)} collective-permute-done((f32[2048,128]{1,0:T(8,128)S(1)}, f32[2048,128]{1,0:T(8,128)S(1)}, u32[]{:S(2)}, u32[]{:S(2)}) %collective-permute-start) | collective-permute-done | bytes 1048608 | tf_op jit(solution)/shard_map/ppermute | solution.py:229
  33.1 0.0 copy-start.5
  33.1 0.0 collective-permute-done.1.high_in
  33.1 0.0 copy-start.6
  33.1 0.0 copy-done
  33.1 1.0 copy-done.5
  34.1 0.3 copy-done.6
  34.4 0.0 copy-start.8
  34.4 49.7 %work.1 = (f32[512,4,128]{2,1,0:T(4,128)}, f32[512,4,128]{2,1,0:T(4,128)}, f32[512,4,128]{2,1,0:T(4,128)}, f32[256,128]{1,0:T(8,128)}) custom-call(s32[2056]{0:T(1024)} %get-tuple-element.12.pidx, s32[264]{0:T(512)} %get-tuple-element.13.order, s32[264]{0:T(512)} %get-tuple-element.14.pos, s32[1]{0:T(128)} %get-tuple-element.15.count, f32[768,128]{1,0:T(8,128)} %bitcast.38, ...), custom_call_target="tpu_custom_call" | custom-call | tf_op jit(solution)/shard_map/work/pallas_call | solution.py:216
  84.2 0.0 copy-start.4
  84.2 0.0 collective-permute-start.3
  84.2 4.8 %collective-permute-start.2 = (f32[512,4,128]{2,1,0:T(4,128)}, f32[512,4,128]{2,1,0:T(4,128)S(1)}, u32[]{:S(2)}, u32[]{:S(2)}) collective-permute-start(f32[512,4,128]{2,1,0:T(4,128)} %get-tuple-element.19), channel_id=1, source_target_pairs={{0,120},{8,0},{16,8},{24,16},{32,24},{40,32},{48,40},{56,48},{64,5... | collective-permute-start | bytes 3145736 | tf_op jit(solution)/shard_map/ppermute | solution.py:229
  89.0 0.0 copy-done.8
  89.0 0.1 convert_element_type.20
  89.1 1.6 %pad_maximum_fusion.1 = f32[8,33,128]{2,1,0:T(8,128)} fusion(f32[8,1,128]{2,1,0:T(1,128)S(1)} %bitcast.40, f32[8,32,128]{2,1,0:T(8,128)} %bitcast.39), kind=kLoop, calls=%fused_computation.15 | loop fusion | flops 33792 | bytes 270336 | tf_op jit(solution)/shard_map/concatenate | solution.py:246
  90.7 5.8 %all-to-all-start = ((f32[8,33,128]{2,1,0:T(8,128)}), f32[8,33,128]{2,1,0:T(8,128)}, u32[]{:S(2)}, u32[]{:S(2)}) async-start(f32[8,33,128]{2,1,0:T(8,128)} %pad_maximum_fusion.1), calls=%async_computation | async-start | bytes 327680 | tf_op jit(solution)/shard_map/all_to_all | solution.py:247
  96.5 5.9 %all-to-all-done = f32[8,33,128]{2,1,0:T(8,128)} async-done(((f32[8,33,128]{2,1,0:T(8,128)}), f32[8,33,128]{2,1,0:T(8,128)}, u32[]{:S(2)}, u32[]{:S(2)}) %all-to-all-start) | async-done | bytes 135200 | tf_op jit(solution)/shard_map/all_to_all | solution.py:247
  102.4 0.8 slice_reduce_fusion
  103.1 0.1 eq.16
  103.2 0.9 slice.35
  104.1 0.9 fusion.7
  105.0 6.7 %collective-permute-done.3 = f32[512,4,128]{2,1,0:T(4,128)S(1)} collective-permute-done((f32[512,4,128]{2,1,0:T(4,128)}, f32[512,4,128]{2,1,0:T(4,128)S(1)}, u32[]{:S(2)}, u32[]{:S(2)}) %collective-permute-start.3) | collective-permute-done | bytes 1048608 | tf_op jit(solution)/shard_map/ppermute | solution.py:229
  111.7 0.0 collective-permute-done.2
  111.7 0.0 copy-done.4
  111.7 0.2 add_add_fusion
  111.9 0.0 copy-start.2
  111.9 0.0 copy-start.7
  111.9 0.2 slice.36
  112.1 0.9 copy-done.7
  113.1 0.7 multiply_add_fusion
  113.8 0.0 copy-done.2
  (3 shorter events, 0.0 us)
Async XLA Ops:
  0.6 1.4 %copy-start.1 = (f32[512,3,128]{2,0,1:T(8,128)S(1)}, f32[512,3,128]{2,0,1:T(8,128)}, u32[]{:S(2)}) copy-start(f32[512,3,128]{2,0,1:T(8,128)} %param.12) | copy-start | bytes 2359300
  2.0 0.9 copy-start.3
  3.1 30.0 %copy-start = (f32[4,512,128]{2,1,0:T(8,128)}, f32[4,512,128]{2,1,0:T(8,128)S(1)}, u32[]{:S(2)}) copy-start(f32[4,512,128]{2,1,0:T(8,128)S(1)} %pad_maximum_fusion) | copy-start | bytes 3145732
  3.1 30.0 %collective-permute-start = (f32[2048,128]{1,0:T(8,128)S(1)}, f32[2048,128]{1,0:T(8,128)S(1)}, u32[]{:S(2)}, u32[]{:S(2)}) collective-permute-start(f32[2048,128]{1,0:T(8,128)S(1)} %bitcast.28), channel_id=1, source_target_pairs={{0,8},{8,16},{16,24},{24,32},{32,40},{40,48},{48,56},{56,64},{64,7... | collective-permute-start | bytes 3145736 | tf_op jit(solution)/shard_map/ppermute | solution.py:229
  5.3 27.8 %collective-permute-start.1 = (f32[2048,128]{1,0:T(8,128)S(1)}, f32[2048,128]{1,0:T(8,128)S(1)}, u32[]{:S(2)}, u32[]{:S(2)}) collective-permute-start(f32[2048,128]{1,0:T(8,128)S(1)} %bitcast.29), channel_id=1, source_target_pairs={{0,120},{8,0},{16,8},{24,16},{32,24},{40,32},{48,40},{56,48},{64,5... | collective-permute-start | bytes 3145736 | tf_op jit(solution)/shard_map/ppermute | solution.py:229
  33.1 1.0 copy-start.5
  33.1 1.3 %copy-start.6 = (f32[2048,128]{1,0:T(8,128)}, f32[2048,128]{1,0:T(8,128)S(1)}, u32[]{:S(2)}) copy-start(f32[2048,128]{1,0:T(8,128)S(1)} %collective-permute-done.1.high_in) | copy-start | bytes 3145732
  34.4 54.5 %copy-start.8 = (s32[264]{0:T(512)S(1)}, s32[264]{0:T(512)}, u32[]{:S(2)}) copy-start(s32[264]{0:T(512)} %get-tuple-element.17) | copy-start | bytes 3172
  84.2 27.6 %copy-start.4 = (f32[512,4,128]{2,1,0:T(4,128)S(1)}, f32[512,4,128]{2,1,0:T(4,128)}, u32[]{:S(2)}) copy-start(f32[512,4,128]{2,1,0:T(4,128)} %get-tuple-element.18) | copy-start | bytes 3145732
  84.2 27.6 %collective-permute-start.3 = (f32[512,4,128]{2,1,0:T(4,128)}, f32[512,4,128]{2,1,0:T(4,128)S(1)}, u32[]{:S(2)}, u32[]{:S(2)}) collective-permute-start(f32[512,4,128]{2,1,0:T(4,128)} %get-tuple-element.20), channel_id=1, source_target_pairs={{0,8},{8,16},{16,24},{24,32},{32,40},{40,48},{48,56},{56,64},{64,7... | collective-permute-start | bytes 3145736 | tf_op jit(solution)/shard_map/ppermute | solution.py:229
  84.2 27.6 %collective-permute-start.2 = (f32[512,4,128]{2,1,0:T(4,128)}, f32[512,4,128]{2,1,0:T(4,128)S(1)}, u32[]{:S(2)}, u32[]{:S(2)}) collective-permute-start(f32[512,4,128]{2,1,0:T(4,128)} %get-tuple-element.19), channel_id=1, source_target_pairs={{0,120},{8,0},{16,8},{24,16},{32,24},{40,32},{48,40},{56,48},{64,5... | collective-permute-start | bytes 3145736 | tf_op jit(solution)/shard_map/ppermute | solution.py:229
  90.7 11.7 %all-to-all-start = ((f32[8,33,128]{2,1,0:T(8,128)}), f32[8,33,128]{2,1,0:T(8,128)}, u32[]{:S(2)}, u32[]{:S(2)}) async-start(f32[8,33,128]{2,1,0:T(8,128)} %pad_maximum_fusion.1), calls=%async_computation | async-start | bytes 327680 | tf_op jit(solution)/shard_map/all_to_all | solution.py:247
  111.9 1.9 %copy-start.2 = (f32[256,8,128]{2,1,0:T(8,128)}, f32[256,8,128]{2,1,0:T(8,128)S(1)}, u32[]{:S(2)}) copy-start(f32[256,8,128]{2,1,0:T(8,128)S(1)} %add_add_fusion) | copy-start | bytes 3145732
  111.9 1.1 %copy-start.7 = (f32[512,128]{1,0:T(8,128)S(1)}, f32[512,128]{1,0:T(8,128)}, u32[]{:S(2)}) copy-start(f32[512,128]{1,0:T(8,128)} %param.14) | copy-start | bytes 786436

commit v3 on v2

v3 whole, which is shorter than its diff:
```python
import math

import jax
import jax.numpy as jnp
from jax import lax
from jax.experimental import pallas as pl
from jax.experimental.pallas import tpu as pltpu
from jax.sharding import PartitionSpec as P

BS = 128
KC = 8
PAIR_CAP = 32
VB = 256
SB = 512
POOL = 3 * SB
N_GX = 16
N_GY = 8
ROWS = 128
GROUP = 40
SLOTS = 4
TOGETHER = 2

EPS = 0.05
STEP = 0.5
LOG2E = math.log2(math.e)
LN2 = math.log(2.0)

VMEM = pl.BlockSpec(memory_space=pltpu.VMEM)
SMEM = pl.BlockSpec(memory_space=pltpu.SMEM)
ANY = pl.BlockSpec(memory_space=pl.ANY)
MESH = pl.DeviceIdType.MESH


def bf(x):
    return x.astype(jnp.bfloat16)


def f32(x):
    return x.astype(jnp.float32)


def meet(peers):
    barrier = pltpu.get_barrier_semaphore()
    for peer in peers:
        pl.semaphore_signal(barrier, inc=1, device_id=peer, device_id_type=MESH)
    pl.semaphore_wait(barrier, len(peers))


def exchange_kernel(
    xyz, pot, cand, home_hbm, own, low, high, pidx, home, home_sem, send_sem, recv_sem
):
    x, g = lax.axis_index("gx"), lax.axis_index("gy")
    below, above = (x + N_GX - 1) % N_GX, (x + 1) % N_GX
    fetch = pltpu.make_async_copy(home_hbm, home, home_sem)
    fetch.start()

    @pl.loop(0, SB // 64)
    def _(i):
        at = pl.multiple_of(i * 64, 64)
        square = None
        for c in range(3):
            y = xyz[c, pl.ds(at, 64), :] - 0.5
            own[pl.ds(c * SB + at, 64), :] = (2.0 * LOG2E / EPS) * y
            square = y * y if square is None else square + y * y
        own[pl.ds(3 * SB + at, 64), :] = LOG2E * (pot[pl.ds(at, 64), :] - (1.0 / EPS) * square)

    meet([(below, g), (above, g)])
    up = pltpu.make_async_remote_copy(
        own, low, send_sem.at[0], recv_sem.at[0], device_id=(above, g), device_id_type=MESH
    )
    down = pltpu.make_async_remote_copy(
        own, high, send_sem.at[1], recv_sem.at[1], device_id=(below, g), device_id_type=MESH
    )
    up.start()
    down.start()
    fetch.wait()

    @pl.loop(0, VB // 2)
    def _(h):
        for u in range(2):
            v = 2 * h + u
            for k in range(KC):
                s = home[cand[k, v]]
                pidx[v * KC + k] = ((((s >> 12) - x + 1) & 15) << 9) | (s & 511)

    up.wait()
    down.wait()


def exchange(xyz, pot, cand, home):
    table = jax.ShapeDtypeStruct((4 * SB, BS), jnp.float32)
    return pl.pallas_call(
        exchange_kernel,
        in_specs=[VMEM, VMEM, SMEM, ANY],
        out_specs=[VMEM] * 3 + [SMEM],
        out_shape=[table] * 3 + [jax.ShapeDtypeStruct((VB * KC,), jnp.int32)],
        scratch_shapes=[
            pltpu.SMEM((N_GX * N_GY * SB,), jnp.int32),
            pltpu.SemaphoreType.DMA(()),
            pltpu.SemaphoreType.DMA((2,)),
            pltpu.SemaphoreType.DMA((2,)),
        ],
        compiler_params=pltpu.CompilerParams(
            collective_id=0, has_side_effects=True, vmem_limit_bytes=32 << 20
        ),
        name="exchange",
    )(xyz, pot, cand, home)


def finish_kernel(
    low, own, high, dual, pot, target, dual_pot, moments, new_pot,
    above_in, below_in, got, dual_send, dual_recv, send_sem, recv_sem,
):
    x, g = lax.axis_index("gx"), lax.axis_index("gy")
    below, above = (x + N_GX - 1) % N_GX, (x + 1) % N_GX
    others = [(g + d) % N_GY for d in range(1, N_GY)]
    meet([(below, g), (above, g)] + [(x, peer) for peer in others])
    down = pltpu.make_async_remote_copy(
        low, above_in, send_sem.at[0], recv_sem.at[0], device_id=(below, g), device_id_type=MESH
    )
    up = pltpu.make_async_remote_copy(
        high, below_in, send_sem.at[1], recv_sem.at[1], device_id=(above, g), device_id_type=MESH
    )
    down.start()
    up.start()
    copies = []
    for d, peer in enumerate(others):
        copy = pltpu.make_async_remote_copy(
            dual.at[peer], got.at[g], dual_send.at[d], dual_recv.at[d],
            device_id=(x, peer), device_id_type=MESH,
        )
        copy.start()
        copies.append(copy)
    got[g] = dual[g]
    for copy in copies:
        copy.wait()
    row = lax.broadcasted_iota(jnp.int32, (ROWS, BS), 0).astype(jnp.float32)
    total = None
    for half in range(2):
        fill = None
        for j in range(4):
            index = got[4 * half + j, PAIR_CAP : PAIR_CAP + 1, :]
            fill = index if fill is None else jnp.maximum(fill, index)
        hot = bf(jnp.where(row == fill, 1.0, 0.0))
        rest = jnp.concatenate([got[4 * half + j, :PAIR_CAP, :] for j in range(4)], axis=0)
        for _ in range(3):
            piece = bf(rest)
            rest = rest - f32(piece)
            term = jnp.dot(hot, piece, preferred_element_type=jnp.float32)
            total = term if total is None else total + term
    dual_pot[...] = total
    down.wait()
    up.wait()

    @pl.loop(0, SB // 16)
    def _(i):
        at = pl.multiple_of(i * 64, 64)
        moments[pl.ds(at, 64), :] = (
            own[pl.ds(at, 64), :] + above_in[pl.ds(at, 64), :] + below_in[pl.ds(at, 64), :]
        )
        for j in range(2):
            rows = pl.ds(pl.multiple_of(i * 16, 16) + 8 * j, 8)
            mass = moments[pl.ds(at + 32 * j, 8, stride=4), :]
            new_pot[rows, :] = pot[rows, :] + STEP * (target[rows, :] - mass)


def finish(low, own, high, dual, pot, target):
    return pl.pallas_call(
        finish_kernel,
        in_specs=[VMEM] * 6,
        out_specs=[VMEM] * 3,
        out_shape=[
            jax.ShapeDtypeStruct((ROWS, BS), jnp.float32),
            jax.ShapeDtypeStruct((4 * SB, BS), jnp.float32),
            jax.ShapeDtypeStruct((SB, BS), jnp.float32),
        ],
        scratch_shapes=[
            pltpu.VMEM((4 * SB, BS), jnp.float32),
            pltpu.VMEM((4 * SB, BS), jnp.float32),
            pltpu.VMEM((N_GY, GROUP, BS), jnp.float32),
            pltpu.SemaphoreType.DMA((N_GY - 1,)),
            pltpu.SemaphoreType.DMA((N_GY - 1,)),
            pltpu.SemaphoreType.DMA((2,)),
            pltpu.SemaphoreType.DMA((2,)),
        ],
        compiler_params=pltpu.CompilerParams(
            collective_id=1, has_side_effects=True, vmem_limit_bytes=32 << 20
        ),
        name="finish",
    )(low, own, high, dual, pot, target)


BUFFERS = ("split", "xat", "part", "top", "f8")


def work_kernel(
    pidx, plan, vox, mass, low_in, own_in, high_in,
    low_out, own_out, high_out, dual, mom, ypool, order, place, ranks, *scratch,
):
    first_lane = (lax.axis_index("gy") & 3) * PAIR_CAP
    for g in range(N_GY):
        ranks[g] = 0

    def compact(h, n):
        for u in range(2):
            v = 2 * h + u
            p = plan[v]
            occupied = (p >= 0).astype(jnp.int32)
            dest = (p >> 7) & 7
            rank = ranks[dest]
            ranks[dest] = rank + occupied
            order[n] = v
            place[n] = (dest << 16) | (rank << 8) | (p & 127)
            n = n + occupied
        return n

    n = lax.fori_loop(0, VB // 2, compact, jnp.int32(0))
    size = len(BUFFERS)
    bufs = [dict(zip(BUFFERS, scratch[i * size : (i + 1) * size])) for i in range(SLOTS * TOGETHER)]
    sub = lax.broadcasted_iota(jnp.int32, (8, BS), 0)
    low = sub < 4
    lane = lax.broadcasted_iota(jnp.int32, (1, BS), 1)
    dual[...] = jnp.full(dual.shape, -1.0, jnp.float32)
    for q, table in enumerate((low_in, own_in, high_in)):

        @pl.loop(0, SB // 16)
        def _(g):
            for j in range(16):
                i = g * 16 + j
                t = table[pl.ds(i, 4, stride=SB), :]
                a = jnp.concatenate([t, t], axis=0)
                hi = f32(bf(a))
                mid = f32(bf(a - hi))
                first = jnp.where(low, hi, mid)
                second = jnp.where(sub == 3, a - hi - mid, jnp.where(sub == 7, 1.0, first))
                ypool[q * SB + i] = bf(jnp.concatenate([first, second], axis=0))
                mom[q * SB + i] = jnp.zeros((8, BS), jnp.float32)

    def prepare(t, b):
        s = order[t]
        x = vox[pl.ds(s, 3, stride=VB), :] - 0.5
        xh = f32(bf(x))
        xl = x - xh
        tops = [f32(ypool[pidx[s * KC + k], 0:8, :]) for k in range(KC)]
        while len(tops) > 1:
            tops = [jnp.maximum(a, c) for a, c in zip(tops[::2], tops[1::2])]
        top = jnp.max(tops[0][3:4], axis=1, keepdims=True)
        top = jnp.broadcast_to(top, (1, BS))
        one = jnp.ones((1, BS), jnp.float32)
        xa = jnp.concatenate([xh, one, xh, one, xl, one, xl, -top], axis=0)
        b["xat"][...] = bf(xa.T)
        b["top"][0:1, :] = top

    def weigh_and_spread(t, b, told, bold):
        part = None
        s = order[t] if t is not None else None
        sold = order[told] if told is not None else None
        for c in range(KC // 2):
            if t is not None:
                y = [ypool[pidx[s * KC + 2 * c + j]] for j in range(2)]
                sc = jnp.dot(
                    b["xat"][...],
                    jnp.concatenate(y, axis=1),
                    preferred_element_type=jnp.float32,
                )
            if told is not None:
                e2 = jnp.concatenate([bold["split"][2 * c], bold["split"][2 * c + 1]], axis=1)
                m = jnp.dot(bold["f8"][...], e2, preferred_element_type=jnp.float32)
                for j in range(2):
                    mom[pidx[sold * KC + 2 * c + j]] += m[:, j * BS : (j + 1) * BS]
            if t is not None:
                e = jnp.exp2(sc)
                eh = bf(e)
                el = bf(e - f32(eh))
                for j in range(2):
                    b["split"][2 * c + j, 0:BS, :] = eh[:, j * BS : (j + 1) * BS]
                    b["split"][2 * c + j, BS:, :] = el[:, j * BS : (j + 1) * BS]
                p = e[:, :BS] + e[:, BS:]
                part = p if part is None else part + p
        if t is not None:
            b["part"][...] = part

    def norm(t, b):
        s = order[t]
        d = jnp.sum(b["part"][...].T, axis=0, keepdims=True)
        xr = vox[pl.ds(s, 3, stride=VB), :]
        x = xr - 0.5
        sq = jnp.sum(x * x, axis=0, keepdims=True)
        where = place[t]
        top_row = (where >> 16) * GROUP
        rank = (where >> 8) & 255
        mark = pl.ds(top_row + PAIR_CAP, 1)
        dual[mark, :] = jnp.where(
            lane == first_lane + rank, (where & 255).astype(jnp.float32), dual[mark, :]
        )
        dual[pl.ds(top_row + rank, 1), :] = (1.0 / EPS) * sq - LN2 * (b["top"][0:1, :] + jnp.log2(d))
        w = mass[pl.ds(s, 1), :] / d
        f = jnp.concatenate([w, xr * w], axis=0)
        fh = f32(bf(f))
        f8 = bf(jnp.concatenate([fh, f - fh], axis=0))
        b["f8"][...] = jnp.concatenate([f8, f8], axis=1)

    def step(g, slot, valid):
        for stage in range(3):
            for u in range(TOGETHER):
                at = lambda lag: (g - lag) * TOGETHER + u if valid(lag) else None
                buf = lambda lag: bufs[((slot - lag) % SLOTS) * TOGETHER + u]
                if stage == 0 and valid(0):
                    prepare(at(0), buf(0))
                if stage == 1 and (valid(1) or valid(3)):
                    weigh_and_spread(at(1), buf(1), at(3), buf(3))
                if stage == 2 and valid(2):
                    norm(at(2), buf(2))

    groups = n // TOGETHER

    @pl.when(n > 0)
    def _():
        for g in range(SLOTS):
            step(g, g, lambda lag: lag <= g)

        @pl.loop(0, (groups - SLOTS) // SLOTS)
        def _(h):
            for u in range(SLOTS):
                step(SLOTS + SLOTS * h + u, u, lambda lag: True)

        for e in range(3):
            step(groups + e, e, lambda lag: lag > e)

    for q, out in enumerate((low_out, own_out, high_out)):

        @pl.loop(0, SB // 16)
        def _(g):
            for j in range(16):
                m = mom[q * SB + g * 16 + j]
                out[g * 16 + j] = m[0:4] + m[4:8]


def work(pidx, plan, vox, mass, low, own, high):
    moments = jax.ShapeDtypeStruct((SB, 4, BS), jnp.float32)
    scratch = [
        pltpu.VMEM((POOL, 8, BS), jnp.float32),
        pltpu.VMEM((POOL, 16, BS), jnp.bfloat16),
        pltpu.SMEM((VB + 8,), jnp.int32),
        pltpu.SMEM((VB + 8,), jnp.int32),
        pltpu.SMEM((N_GY,), jnp.int32),
    ]
    scratch += [
        pltpu.VMEM((KC, 2 * BS, BS), jnp.bfloat16),
        pltpu.VMEM((BS, 16), jnp.bfloat16),
        pltpu.VMEM((BS, BS), jnp.float32),
        pltpu.VMEM((8, BS), jnp.float32),
        pltpu.VMEM((8, 2 * BS), jnp.bfloat16),
    ] * (SLOTS * TOGETHER)
    return pl.pallas_call(
        work_kernel,
        in_specs=[SMEM] * 2 + [VMEM] * 5,
        out_specs=[VMEM] * 4,
        out_shape=[moments] * 3 + [jax.ShapeDtypeStruct((N_GY * GROUP, BS), jnp.float32)],
        scratch_shapes=scratch,
        compiler_params=pltpu.CompilerParams(vmem_limit_bytes=56 << 20),
        name="work",
    )(pidx, plan, vox, mass, low, own, high)


def on_device(
    voxel_xyz, voxel_mass, candidates, offload_plan, seed_xyz, seed_pot, seed_target, seed_home
):
    own_in, low_in, high_in, pidx = exchange(
        jnp.transpose(seed_xyz, (1, 0, 2)), seed_pot, candidates.T, seed_home
    )
    vox = jnp.transpose(voxel_xyz, (1, 0, 2)).reshape(3 * VB, BS)
    low, own, high, dual = work(pidx, offload_plan, vox, voxel_mass, low_in, own_in, high_in)
    flat = lambda m: m.reshape(4 * SB, BS)
    dual_pot, moments, new_pot = finish(
        flat(low), flat(own), flat(high), dual.reshape(N_GY, GROUP, BS), seed_pot, seed_target
    )
    return (dual_pot, moments.reshape(SB, 4, BS), new_pot)


def solution(mesh):
    return jax.shard_map(
        on_device,
        mesh=mesh,
        in_specs=(
            P(("gx", "gy"), None, None),
            P(("gx", "gy"), None),
            P(("gx", "gy"), None),
            P(("gx", "gy")),
            P(("gx", "gy"), None, None),
            P(("gx", "gy"), None),
            P(("gx", "gy"), None),
            P(),
        ),
        out_specs=(P(("gx", "gy"), None), P(("gx", "gy"), None, None), P(("gx", "gy"), None)),
        check_vma=False,
    )
```

time: 114 us -> 131 us (1.15)
  Pallas kernels: 65.2 us -> 116 us
  waiting for transfers between devices: 19.9 us -> 0 us
  starting transfers between devices: 17.8 us -> 0 us
  local copies, waits for them, and re-layouts: 5.27 us -> 14.1 us
  other arithmetic: 3.99 us -> 0 us
    pallas_call x2 -> x3, Pallas kernels: 65.2 us -> 116 us  [the longest x1 72.8 us: finish(): pl.pallas_call(finish_kernel, in_specs=[VMEM] * 6, out_specs=[VMEM] * 3,...]
    ppermute x4 -> x0, waiting for transfers between devices: 14 us -> none  [shifted(): return lax.ppermute(value, 'gx', pairs)]
    ppermute x4 -> x0, starting transfers between devices: 12 us -> none  [shifted(): return lax.ppermute(value, 'gx', pairs)]
    unnamed x18 -> x31, local copies, waits for them, and re-layouts: 3.23 us -> 14.1 us
    all_to_all x1 -> x0, waiting for transfers between devices: 5.87 us -> none  [on_device(): got = lax.all_to_all(send, 'gy', split_axis=0, concat_axis=0, tiled=True)]
    all_to_all x1 -> x0, starting transfers between devices: 5.83 us -> none  [on_device(): got = lax.all_to_all(send, 'gy', split_axis=0, concat_axis=0, tiled=True)]
    slice x3 -> x0, local copies, waits for them, and re-layouts: 1.87 us -> none  [the longest x1 0.91 us: on_device(): got[:, :PAIR_CAP].reshape(-1, BS)]
    concatenate x2 -> x0, other arithmetic: 1.65 us -> none  [the longest x1 1.58 us: on_device(): send = jnp.concatenate([dual.reshape(N_GY, PAIR_CAP, BS), index], axis=1)]
  transfers between devices with their start and end apart: 5 -> 0, of which waited for: 3 -> 0; matrix products, arithmetic and copies ran while one was open for 4% -> 0% of each run, Pallas kernels for 14% -> 0%
where the time goes in v3:
time: 131 us
  Pallas kernels  116 us (89%)
  local copies, waits for them, and re-layouts  14.1 us (11%)
    pallas_call x1, Pallas kernels, finish(): pl.pallas_call(finish_kernel, in_specs=[VMEM] * 6, out_specs=[VMEM] * 3,...  72.8 us
    pallas_call x1, Pallas kernels, exchange(): pl.pallas_call(exchange_kernel, in_specs=[VMEM, VMEM, SMEM, ANY], out_spe...  31.7 us
    unnamed x31, local copies, waits for them, and re-layouts  14.1 us
    pallas_call x1, Pallas kernels, work(): pl.pallas_call(work_kernel, in_specs=[SMEM] * 2 + [VMEM] * 5, out_specs=[...  11.2 us

profile of v3, /device:TPU:1, one launch (start us, length us, event | category | flops | bytes accessed | tf_op | source)
XLA Modules:
  0.0 130.5 jit_solution(803101246152326600)
XLA Ops:
  0.6 0.0 copy-start.6
  0.6 0.9 copy-done.6
  1.6 0.0 copy-start.8
  1.6 1.1 copy-done.8
  2.7 0.0 copy-start.9
  2.7 0.9 copy-done.9
  3.7 0.0 copy-start.12
  3.7 0.7 copy-done.12
  4.4 31.7 %exchange.1 = (f32[2048,128]{1,0:T(8,128)S(1)}, f32[2048,128]{1,0:T(8,128)S(1)}, f32[2048,128]{1,0:T(8,128)S(1)}, s32[2048]{0:T(1024)S(1)}) custom-call(f32[3,512,128]{2,1,0:T(8,128)S(1)} %bitcast.14, f32[512,128]{1,0:T(8,128)S(1)} %copy-done.6, s32[8,256]{1,0:T(8,128)S(1)} %bitcast.16, s32[65536]{0:T(1024)S(1)} %copy-done.9), custom_call_target="tpu_custom_call" | custom-call | tf_op jit(solution)/shard_map/exchange/pallas_call | solution.py:92
  36.0 0.0 copy-start.3
  36.1 1.0 copy-done.3
  37.0 0.0 copy-start.4
  37.0 1.0 copy-done.4
  38.0 0.0 copy-start.5
  38.0 1.0 copy-done.5
  39.0 0.0 copy-start.13
  39.0 0.6 copy-done.13
  39.6 0.0 copy-start.7
  39.6 0.0 copy-start.10
  39.6 11.2 %work.1 = (f32[512,4,128]{2,1,0:T(4,128)}, f32[512,4,128]{2,1,0:T(4,128)}, f32[512,4,128]{2,1,0:T(4,128)}, f32[320,128]{1,0:T(8,128)}) custom-call(s32[2048]{0:T(1024)} %copy-done.13, s32[256]{0:T(256)} %plan.1, f32[768,128]{1,0:T(8,128)} %bitcast.17, f32[256,128]{1,0:T(8,128)} %mass.1, f32[2048,128]{1,0:T(8,128)} %copy-done.4, f32[2048,128]{1,0:T(8,128)} %copy-done.3, ...), custom_call_target="tpu_custom_call" | custom-call | tf_op jit(solution)/shard_map/work/pallas_call | solution.py:355
  50.8 0.0 copy-done.7
  50.8 0.0 copy-done.10
  50.8 0.0 copy-start
  50.8 1.2 copy-done
  52.0 0.0 copy-start.1
  52.0 1.2 copy-done.1
  53.2 0.0 copy-start.2
  53.2 1.2 copy-done.2
  54.4 0.0 copy-start.11
  54.4 0.9 copy-done.11
  55.4 72.8 %finish.1 = (f32[128,128]{1,0:T(8,128)S(1)}, f32[2048,128]{1,0:T(8,128)S(1)}, f32[512,128]{1,0:T(8,128)S(1)}) custom-call(f32[2048,128]{1,0:T(8,128)S(1)} %bitcast.11, f32[2048,128]{1,0:T(8,128)S(1)} %bitcast.12, f32[2048,128]{1,0:T(8,128)S(1)} %bitcast.13, f32[8,40,128]{2,1,0:T(8,128)S(1)} %bitcast.15, f32[512,128]{1,0:T(8,128)S(1)} %copy-done.7, ...), custom_call_target="tpu_custom_call" | custom-call | tf_op jit(solution)/shard_map/finish/pallas_call | solution.py:168
  128.2 0.6 copy.14
  128.9 1.0 copy.15
  129.8 0.7 copy.16
Async XLA Ops:
  0.6 1.0 copy-start.6
  1.6 1.1 copy-start.8
  2.7 0.9 copy-start.9
  3.7 0.7 copy-start.12
  36.0 1.0 copy-start.3
  37.0 1.0 copy-start.4
  38.0 1.0 copy-start.5
  39.0 0.6 copy-start.13
  39.6 11.2 %copy-start.7 = (f32[512,128]{1,0:T(8,128)S(1)}, f32[512,128]{1,0:T(8,128)}, u32[]{:S(2)}) copy-start(f32[512,128]{1,0:T(8,128)} %pot.3) | copy-start | bytes 786436
  39.6 11.2 %copy-start.10 = (f32[512,128]{1,0:T(8,128)S(1)}, f32[512,128]{1,0:T(8,128)}, u32[]{:S(2)}) copy-start(f32[512,128]{1,0:T(8,128)} %target.1) | copy-start | bytes 786436
  50.8 1.2 copy-start
  52.0 1.2 copy-start.1
  53.2 1.2 copy-start.2
  54.4 0.9 copy-start.11

commit v4 on v3

--- a/solution.py
+++ b/solution.py
@@ -27,7 +27,7 @@
 
 VMEM = pl.BlockSpec(memory_space=pltpu.VMEM)
 SMEM = pl.BlockSpec(memory_space=pltpu.SMEM)
-ANY = pl.BlockSpec(memory_space=pl.ANY)
+HBM = pl.BlockSpec(memory_space=pltpu.HBM)
 MESH = pl.DeviceIdType.MESH
 
 
@@ -47,12 +47,17 @@
 
 
 def exchange_kernel(
-    xyz, pot, cand, home_hbm, own, low, high, pidx, home, home_sem, send_sem, recv_sem
+    xyz_hbm, pot_hbm, cand_hbm, home_hbm, own, low, high, pidx,
+    xyz, pot, cand, home, load_sem, send_sem, recv_sem,
 ):
     x, g = lax.axis_index("gx"), lax.axis_index("gy")
     below, above = (x + N_GX - 1) % N_GX, (x + 1) % N_GX
-    fetch = pltpu.make_async_copy(home_hbm, home, home_sem)
-    fetch.start()
+    pairs = ((xyz_hbm, xyz), (pot_hbm, pot), (cand_hbm, cand), (home_hbm, home))
+    loads = [pltpu.make_async_copy(a, b, load_sem.at[i]) for i, (a, b) in enumerate(pairs)]
+    for load in loads:
+        load.start()
+    loads[0].wait()
+    loads[1].wait()
 
     @pl.loop(0, SB // 64)
     def _(i):
@@ -73,7 +78,8 @@
     )
     up.start()
     down.start()
-    fetch.wait()
+    loads[2].wait()
+    loads[3].wait()
 
     @pl.loop(0, VB // 2)
     def _(h):
@@ -91,49 +97,104 @@
     table = jax.ShapeDtypeStruct((4 * SB, BS), jnp.float32)
     return pl.pallas_call(
         exchange_kernel,
-        in_specs=[VMEM, VMEM, SMEM, ANY],
+        in_specs=[HBM] * 4,
         out_specs=[VMEM] * 3 + [SMEM],
         out_shape=[table] * 3 + [jax.ShapeDtypeStruct((VB * KC,), jnp.int32)],
         scratch_shapes=[
+            pltpu.VMEM((3, SB, BS), jnp.float32),
+            pltpu.VMEM((SB, BS), jnp.float32),
+            pltpu.SMEM((KC, VB), jnp.int32),
             pltpu.SMEM((N_GX * N_GY * SB,), jnp.int32),
-            pltpu.SemaphoreType.DMA(()),
+            pltpu.SemaphoreType.DMA((4,)),
             pltpu.SemaphoreType.DMA((2,)),
             pltpu.SemaphoreType.DMA((2,)),
         ],
         compiler_params=pltpu.CompilerParams(
-            collective_id=0, has_side_effects=True, vmem_limit_bytes=32 << 20
+            collective_id=0, has_side_effects=True, vmem_limit_bytes=16 << 20
         ),
         name="exchange",
-    )(xyz, pot, cand, home)
-
-
-def finish_kernel(
-    low, own, high, dual, pot, target, dual_pot, moments, new_pot,
-    above_in, below_in, got, dual_send, dual_recv, send_sem, recv_sem,
+    )(*(pltpu.with_memory_space_constraint(a, pltpu.HBM) for a in (xyz, pot, cand, home)))
+
+
+def deliver_kernel(
+    low, high, dual, above_in, below_in, got, dual_send, dual_recv, send_sem, recv_sem, own_sem
 ):
     x, g = lax.axis_index("gx"), lax.axis_index("gy")
     below, above = (x + N_GX - 1) % N_GX, (x + 1) % N_GX
     others = [(g + d) % N_GY for d in range(1, N_GY)]
     meet([(below, g), (above, g)] + [(x, peer) for peer in others])
-    down = pltpu.make_async_remote_copy(
-        low, above_in, send_sem.at[0], recv_sem.at[0], device_id=(below, g), device_id_type=MESH
-    )
-    up = pltpu.make_async_remote_copy(
-        high, below_in, send_sem.at[1], recv_sem.at[1], device_id=(above, g), device_id_type=MESH
-    )
-    down.start()
-    up.start()
-    copies = []
+    copies = [
+        pltpu.make_async_remote_copy(
+            low, above_in, send_sem.at[0], recv_sem.at[0],
+            device_id=(below, g), device_id_type=MESH,
+        ),
+        pltpu.make_async_remote_copy(
+            high, below_in, send_sem.at[1], recv_sem.at[1],
+            device_id=(above, g), device_id_type=MESH,
+        ),
+    ]
     for d, peer in enumerate(others):
-        copy = pltpu.make_async_remote_copy(
-            dual.at[peer], got.at[g], dual_send.at[d], dual_recv.at[d],
-            device_id=(x, peer), device_id_type=MESH,
+        copies.append(
+            pltpu.make_async_remote_copy(
+                dual.at[peer], got.at[g], dual_send.at[d], dual_recv.at[d],
+                device_id=(x, peer), device_id_type=MESH,
+            )
         )
+    keep = pltpu.make_async_copy(dual.at[g], got.at[g], own_sem)
+    for copy in copies:
         copy.start()
-        copies.append(copy)
-    got[g] = dual[g]
+    keep.start()
+    keep.wait()
     for copy in copies:
         copy.wait()
+
+
+def deliver(low, high, dual):
+    moments = jax.ShapeDtypeStruct((4 * SB, BS), jnp.float32)
+    return pl.pallas_call(
+        deliver_kernel,
+        in_specs=[VMEM] * 3,
+        out_specs=[VMEM] * 3,
+        out_shape=[moments] * 2 + [jax.ShapeDtypeStruct((N_GY, GROUP, BS), jnp.float32)],
+        scratch_shapes=[
+            pltpu.SemaphoreType.DMA((N_GY - 1,)),
+            pltpu.SemaphoreType.DMA((N_GY - 1,)),
+            pltpu.SemaphoreType.DMA((2,)),
+            pltpu.SemaphoreType.DMA((2,)),
+            pltpu.SemaphoreType.DMA(()),
+        ],
+        compiler_params=pltpu.CompilerParams(
+            collective_id=1, has_side_effects=True, vmem_limit_bytes=16 << 20
+        ),
+        name="deliver",
+    )(low, high, dual)
+
+
+def total_kernel(
+    own, above_in, below_in, got, pot, target, dual_hbm, moments_hbm, new_pot_hbm,
+    moments, new_pot, dual_pot, sems,
+):
+    parts = 4
+    size = 4 * SB // parts
+    sends = []
+    for q in range(parts):
+
+        @pl.loop(0, SB // 16 // parts)
+        def _(i):
+            at = pl.multiple_of(q * size + i * 64, 64)
+            moments[pl.ds(at, 64), :] = (
+                own[pl.ds(at, 64), :] + above_in[pl.ds(at, 64), :] + below_in[pl.ds(at, 64), :]
+            )
+            for j in range(2):
+                rows = pl.ds(pl.multiple_of(q * (size // 4) + i * 16, 16) + 8 * j, 8)
+                mass = moments[pl.ds(at + 32 * j, 8, stride=4), :]
+                new_pot[rows, :] = pot[rows, :] + STEP * (target[rows, :] - mass)
+
+        some = pl.ds(q * size, size)
+        sends.append(pltpu.make_async_copy(moments.at[some], moments_hbm.at[some], sems.at[q]))
+        sends[-1].start()
+    sends.append(pltpu.make_async_copy(new_pot, new_pot_hbm, sems.at[parts]))
+    sends[-1].start()
     row = lax.broadcasted_iota(jnp.int32, (ROWS, BS), 0).astype(jnp.float32)
     total = None
     for half in range(2):
@@ -149,45 +210,28 @@
             term = jnp.dot(hot, piece, preferred_element_type=jnp.float32)
             total = term if total is None else total + term
     dual_pot[...] = total
-    down.wait()
-    up.wait()
-
-    @pl.loop(0, SB // 16)
-    def _(i):
-        at = pl.multiple_of(i * 64, 64)
-        moments[pl.ds(at, 64), :] = (
-            own[pl.ds(at, 64), :] + above_in[pl.ds(at, 64), :] + below_in[pl.ds(at, 64), :]
-        )
-        for j in range(2):
-            rows = pl.ds(pl.multiple_of(i * 16, 16) + 8 * j, 8)
-            mass = moments[pl.ds(at + 32 * j, 8, stride=4), :]
-            new_pot[rows, :] = pot[rows, :] + STEP * (target[rows, :] - mass)
-
-
-def finish(low, own, high, dual, pot, target):
+    sends.append(pltpu.make_async_copy(dual_pot, dual_hbm, sems.at[parts + 1]))
+    sends[-1].start()
+    for send in sends:
+        send.wait()
+
+
+def total(own, above_in, below_in, got, pot, target):
+    shapes = [(ROWS, BS), (4 * SB, BS), (SB, BS)]
     return pl.pallas_call(
-        finish_kernel,
+        total_kernel,
         in_specs=[VMEM] * 6,
-        out_specs=[VMEM] * 3,
-        out_shape=[
-            jax.ShapeDtypeStruct((ROWS, BS), jnp.float32),
-            jax.ShapeDtypeStruct((4 * SB, BS), jnp.float32),
-            jax.ShapeDtypeStruct((SB, BS), jnp.float32),
-        ],
+        out_specs=[HBM] * 3,
+        out_shape=[jax.ShapeDtypeStruct(shape, jnp.float32) for shape in shapes],
         scratch_shapes=[
             pltpu.VMEM((4 * SB, BS), jnp.float32),
-            pltpu.VMEM((4 * SB, BS), jnp.float32),
-            pltpu.VMEM((N_GY, GROUP, BS), jnp.float32),
-            pltpu.SemaphoreType.DMA((N_GY - 1,)),
-            pltpu.SemaphoreType.DMA((N_GY - 1,)),
-            pltpu.SemaphoreType.DMA((2,)),
-            pltpu.SemaphoreType.DMA((2,)),
+            pltpu.VMEM((SB, BS), jnp.float32),
+            pltpu.VMEM((ROWS, BS), jnp.float32),
+            pltpu.SemaphoreType.DMA((6,)),
         ],
-        compiler_params=pltpu.CompilerParams(
-            collective_id=1, has_side_effects=True, vmem_limit_bytes=32 << 20
-        ),
-        name="finish",
-    )(low, own, high, dual, pot, target)
+        compiler_params=pltpu.CompilerParams(vmem_limit_bytes=16 << 20),
+        name="total",
+    )(own, above_in, below_in, got, pot, target)
 
 
 BUFFERS = ("split", "xat", "part", "top", "f8")
@@ -358,7 +402,7 @@
         out_specs=[VMEM] * 4,
         out_shape=[moments] * 3 + [jax.ShapeDtypeStruct((N_GY * GROUP, BS), jnp.float32)],
         scratch_shapes=scratch,
-        compiler_params=pltpu.CompilerParams(vmem_limit_bytes=56 << 20),
+        compiler_params=pltpu.CompilerParams(vmem_limit_bytes=32 << 20),
         name="work",
     )(pidx, plan, vox, mass, low, own, high)
 
@@ -372,8 +416,9 @@
     vox = jnp.transpose(voxel_xyz, (1, 0, 2)).reshape(3 * VB, BS)
     low, own, high, dual = work(pidx, offload_plan, vox, voxel_mass, low_in, own_in, high_in)
     flat = lambda m: m.reshape(4 * SB, BS)
-    dual_pot, moments, new_pot = finish(
-        flat(low), flat(own), flat(high), dual.reshape(N_GY, GROUP, BS), seed_pot, seed_target
+    above_in, below_in, got = deliver(flat(low), flat(high), dual.reshape(N_GY, GROUP, BS))
+    dual_pot, moments, new_pot = total(
+        flat(own), above_in, below_in, got, seed_pot, seed_target
     )
     return (dual_pot, moments.reshape(SB, 4, BS), new_pot)
 

time: 131 us -> 116 us (0.89)
  local copies, waits for them, and re-layouts: 14.1 us -> 0.68 us
  Pallas kernels: 116 us -> 114 us
    pallas_call x2 -> x3, Pallas kernels: 105 us -> 65.6 us  [the longest x1 32.3 us: exchange(): pl.pallas_call(exchange_kernel, in_specs=[HBM] * 4, out_specs=[VMEM] * 3...]
    pallas_call x1, Pallas kernels: 11.2 us -> 48.4 us  [work(): pl.pallas_call(work_kernel, in_specs=[SMEM] * 2 + [VMEM] * 5, out_specs=[...]
    unnamed x31 -> x10, local copies, waits for them, and re-layouts: 14.1 us -> 0.68 us
where the time goes in v4:
time: 116 us; the launch traced here: 115 us
  Pallas kernels  114 us (98%)
    pallas_call x1, Pallas kernels, work(): pl.pallas_call(work_kernel, in_specs=[SMEM] * 2 + [VMEM] * 5, out_specs=[...  48.4 us
    pallas_call x1, Pallas kernels, exchange(): pl.pallas_call(exchange_kernel, in_specs=[HBM] * 4, out_specs=[VMEM] * 3...  32.3 us
    pallas_call x1, Pallas kernels, deliver(): pl.pallas_call(deliver_kernel, in_specs=[VMEM] * 3, out_specs=[VMEM] * 3,...  32 us

profile of v4, /device:TPU:1, one launch (start us, length us, event | category | flops | bytes accessed | tf_op | source)
XLA Modules:
  0.0 115.4 jit_solution(13405220051841489883)
XLA Ops:
  0.6 0.0 copy-start.1
  0.6 0.0 copy-start.3
  0.7 32.3 %exchange.1 = (f32[2048,128]{1,0:T(8,128)S(1)}, f32[2048,128]{1,0:T(8,128)S(1)}, f32[2048,128]{1,0:T(8,128)S(1)}, s32[2048]{0:T(1024)S(1)}) custom-call(f32[3,512,128]{2,1,0:T(8,128)} %bitcast.15, f32[512,128]{1,0:T(8,128)} %pot.1, s32[8,256]{1,0:T(8,128)} %bitcast.16, s32[65536]{0:T(1024)} %home_hbm.1), custom_call_target="tpu_custom_call" | custom-call | tf_op jit(solution)/shard_map/exchange/pallas_call | solution.py:98
  32.9 0.0 copy-start.4
  32.9 0.0 copy-done.1
  32.9 0.0 copy-done.3
  32.9 0.7 copy-done.4
  33.6 48.4 %work.1 = (f32[512,4,128]{2,1,0:T(4,128)S(1)}, f32[512,4,128]{2,1,0:T(4,128)S(1)}, f32[512,4,128]{2,1,0:T(4,128)S(1)}, f32[320,128]{1,0:T(8,128)S(1)}) custom-call(s32[2048]{0:T(1024)S(1)} %get-tuple-element.17.pidx, s32[256]{0:T(256)S(1)} %copy-done.4, f32[768,128]{1,0:T(8,128)S(1)} %bitcast.13, f32[256,128]{1,0:T(8,128)S(1)} %copy-done.3, ...), custom_call_target="tpu_custom_call" | custom-call | tf_op jit(solution)/shard_map/work/pallas_call | solution.py:399
  82.0 0.0 copy-start
  82.0 0.0 copy-start.2
  82.1 32.0 %deliver.1 = (f32[2048,128]{1,0:T(8,128)S(1)}, f32[2048,128]{1,0:T(8,128)S(1)}, f32[8,40,128]{2,1,0:T(8,128)S(1)}) custom-call(f32[2048,128]{1,0:T(8,128)S(1)} %bitcast.10, f32[2048,128]{1,0:T(8,128)S(1)} %bitcast.11, f32[8,40,128]{2,1,0:T(8,128)S(1)} %bitcast.14), custom_call_target="tpu_custom_call" | custom-call | tf_op jit(solution)/shard_map/deliver/pallas_call | solution.py:154
  114.1 0.0 copy-done
  114.1 0.0 copy-done.2
  114.1 1.4 %total.1 = (f32[128,128]{1,0:T(8,128)}, f32[2048,128]{1,0:T(8,128)}, f32[512,128]{1,0:T(8,128)}) custom-call(f32[2048,128]{1,0:T(8,128)S(1)} %bitcast.12, f32[2048,128]{1,0:T(8,128)S(1)} %get-tuple-element.25.above_in, f32[2048,128]{1,0:T(8,128)S(1)} %get-tuple-element.26.below_in, f32[8,40,128]{2,1,0:T(8,128)S(1)} %get-tuple-element.27.got, ...), custom_call_target="tpu_custom_call" | custom-call | tf_op jit(solution)/shard_map/total/pallas_call | solution.py:221
Async XLA Ops:
  0.6 32.3 %copy-start.1 = (f32[256,3,128]{2,0,1:T(8,128)S(1)}, f32[256,3,128]{2,0,1:T(8,128)}, u32[]{:S(2)}) copy-start(f32[256,3,128]{2,0,1:T(8,128)} %param.8) | copy-start | bytes 1179652
  0.6 32.3 %copy-start.3 = (f32[256,128]{1,0:T(8,128)S(1)}, f32[256,128]{1,0:T(8,128)}, u32[]{:S(2)}) copy-start(f32[256,128]{1,0:T(8,128)} %mass.1) | copy-start | bytes 393220
  32.9 0.7 copy-start.4
  82.0 32.0 %copy-start = (f32[512,128]{1,0:T(8,128)S(1)}, f32[512,128]{1,0:T(8,128)}, u32[]{:S(2)}) copy-start(f32[512,128]{1,0:T(8,128)} %pot.1) | copy-start | bytes 786436
  82.0 32.0 %copy-start.2 = (f32[512,128]{1,0:T(8,128)S(1)}, f32[512,128]{1,0:T(8,128)}, u32[]{:S(2)}) copy-start(f32[512,128]{1,0:T(8,128)} %target.1) | copy-start | bytes 786436

commit v5 on v4

--- a/solution.py
+++ b/solution.py
@@ -19,6 +19,7 @@
 GROUP = 40
 SLOTS = 4
 TOGETHER = 2
+CHUNKS = 4
 
 EPS = 0.05
 STEP = 0.5
@@ -47,37 +48,61 @@
 
 
 def exchange_kernel(
-    xyz_hbm, pot_hbm, cand_hbm, home_hbm, own, low, high, pidx,
-    xyz, pot, cand, home, load_sem, send_sem, recv_sem,
+    xyz_hbm, pot_hbm, cand_hbm, home_hbm, ypool, pidx,
+    xyz, pot, plane, cand, home, load_sem, send_sem, recv_sem,
 ):
     x, g = lax.axis_index("gx"), lax.axis_index("gy")
     below, above = (x + N_GX - 1) % N_GX, (x + 1) % N_GX
-    pairs = ((xyz_hbm, xyz), (pot_hbm, pot), (cand_hbm, cand), (home_hbm, home))
+    pairs = (
+        (xyz_hbm, xyz.at[1]), (pot_hbm, pot.at[1]), (cand_hbm, cand), (home_hbm, home)
+    )
     loads = [pltpu.make_async_copy(a, b, load_sem.at[i]) for i, (a, b) in enumerate(pairs)]
     for load in loads:
         load.start()
+    meet([(below, g), (above, g)])
+    copies = []
+    for q in range(CHUNKS):
+        some = pl.ds(q * (SB // CHUNKS), SB // CHUNKS)
+        for way, (slot, peer) in enumerate(((0, above), (2, below))):
+            for kind, (source, dest) in enumerate(
+                (
+                    (xyz_hbm.at[:, some, :], xyz.at[slot, :, some, :]),
+                    (pot_hbm.at[some, :], pot.at[slot, some, :]),
+                )
+            ):
+                i = (q * 2 + way) * 2 + kind
+                copy = pltpu.make_async_remote_copy(
+                    source, dest, send_sem.at[i], recv_sem.at[i],
+                    device_id=(peer, g), device_id_type=MESH,
+                )
+                copy.start()
+                copies.append(copy)
+
+    sub = lax.broadcasted_iota(jnp.int32, (8, BS), 0)
+    low = sub < 4
+
+    def build(slot, start, count):
+        @pl.loop(0, count // 16)
+        def _(i):
+            at = pl.multiple_of(start + i * 16, 16)
+            square = None
+            for c in range(3):
+                y = xyz[slot, c, pl.ds(at, 16), :] - 0.5
+                plane[c * 16 : (c + 1) * 16, :] = (2.0 * LOG2E / EPS) * y
+                square = y * y if square is None else square + y * y
+            plane[48:64, :] = LOG2E * (pot[slot, pl.ds(at, 16), :] - (1.0 / EPS) * square)
+            for j in range(16):
+                t = plane[pl.ds(j, 4, stride=16), :]
+                a = jnp.concatenate([t, t], axis=0)
+                hi = f32(bf(a))
+                mid = f32(bf(a - hi))
+                first = jnp.where(low, hi, mid)
+                second = jnp.where(sub == 3, a - hi - mid, jnp.where(sub == 7, 1.0, first))
+                ypool[slot * SB + at + j] = bf(jnp.concatenate([first, second], axis=0))
+
     loads[0].wait()
     loads[1].wait()
-
-    @pl.loop(0, SB // 64)
-    def _(i):
-        at = pl.multiple_of(i * 64, 64)
-        square = None
-        for c in range(3):
-            y = xyz[c, pl.ds(at, 64), :] - 0.5
-            own[pl.ds(c * SB + at, 64), :] = (2.0 * LOG2E / EPS) * y
-            square = y * y if square is None else square + y * y
-        own[pl.ds(3 * SB + at, 64), :] = LOG2E * (pot[pl.ds(at, 64), :] - (1.0 / EPS) * square)
-
-    meet([(below, g), (above, g)])
-    up = pltpu.make_async_remote_copy(
-        own, low, send_sem.at[0], recv_sem.at[0], device_id=(above, g), device_id_type=MESH
-    )
-    down = pltpu.make_async_remote_copy(
-        own, high, send_sem.at[1], recv_sem.at[1], device_id=(below, g), device_id_type=MESH
-    )
-    up.start()
-    down.start()
+    build(1, 0, SB)
     loads[2].wait()
     loads[3].wait()
 
@@ -89,25 +114,33 @@
                 s = home[cand[k, v]]
                 pidx[v * KC + k] = ((((s >> 12) - x + 1) & 15) << 9) | (s & 511)
 
-    up.wait()
-    down.wait()
+    for q in range(CHUNKS):
+        for copy in copies[4 * q : 4 * q + 4]:
+            copy.wait_recv()
+        for slot in (0, 2):
+            build(slot, q * (SB // CHUNKS), SB // CHUNKS)
+    for copy in copies:
+        copy.wait_send()
 
 
 def exchange(xyz, pot, cand, home):
-    table = jax.ShapeDtypeStruct((4 * SB, BS), jnp.float32)
     return pl.pallas_call(
         exchange_kernel,
         in_specs=[HBM] * 4,
-        out_specs=[VMEM] * 3 + [SMEM],
-        out_shape=[table] * 3 + [jax.ShapeDtypeStruct((VB * KC,), jnp.int32)],
+        out_specs=[VMEM, SMEM],
+        out_shape=[
+            jax.ShapeDtypeStruct((POOL, 16, BS), jnp.bfloat16),
+            jax.ShapeDtypeStruct((VB * KC,), jnp.int32),
+        ],
         scratch_shapes=[
+            pltpu.VMEM((3, 3, SB, BS), jnp.float32),
             pltpu.VMEM((3, SB, BS), jnp.float32),
-            pltpu.VMEM((SB, BS), jnp.float32),
+            pltpu.VMEM((64, BS), jnp.float32),
             pltpu.SMEM((KC, VB), jnp.int32),
             pltpu.SMEM((N_GX * N_GY * SB,), jnp.int32),
             pltpu.SemaphoreType.DMA((4,)),
-            pltpu.SemaphoreType.DMA((2,)),
-            pltpu.SemaphoreType.DMA((2,)),
+            pltpu.SemaphoreType.DMA((4 * CHUNKS,)),
+            pltpu.SemaphoreType.DMA((4 * CHUNKS,)),
         ],
         compiler_params=pltpu.CompilerParams(
             collective_id=0, has_side_effects=True, vmem_limit_bytes=16 << 20
@@ -238,9 +271,15 @@
 
 
 def work_kernel(
-    pidx, plan, vox, mass, low_in, own_in, high_in,
-    low_out, own_out, high_out, dual, mom, ypool, order, place, ranks, *scratch,
+    pidx, plan, vox_hbm, mass_hbm, ypool,
+    low_out, own_out, high_out, dual, mom, vox, mass, sems, order, place, ranks, *scratch,
 ):
+    loads = [
+        pltpu.make_async_copy(vox_hbm, vox, sems.at[0]),
+        pltpu.make_async_copy(mass_hbm, mass, sems.at[1]),
+    ]
+    for load in loads:
+        load.start()
     first_lane = (lax.axis_index("gy") & 3) * PAIR_CAP
     for g in range(N_GY):
         ranks[g] = 0
@@ -256,29 +295,17 @@
             order[n] = v
             place[n] = (dest << 16) | (rank << 8) | (p & 127)
             n = n + occupied
+            for j in range(POOL // VB):
+                mom[v * (POOL // VB) + j] = jnp.zeros((8, BS), jnp.float32)
         return n
 
     n = lax.fori_loop(0, VB // 2, compact, jnp.int32(0))
+    for load in loads:
+        load.wait()
     size = len(BUFFERS)
     bufs = [dict(zip(BUFFERS, scratch[i * size : (i + 1) * size])) for i in range(SLOTS * TOGETHER)]
-    sub = lax.broadcasted_iota(jnp.int32, (8, BS), 0)
-    low = sub < 4
     lane = lax.broadcasted_iota(jnp.int32, (1, BS), 1)
     dual[...] = jnp.full(dual.shape, -1.0, jnp.float32)
-    for q, table in enumerate((low_in, own_in, high_in)):
-
-        @pl.loop(0, SB // 16)
-        def _(g):
-            for j in range(16):
-                i = g * 16 + j
-                t = table[pl.ds(i, 4, stride=SB), :]
-                a = jnp.concatenate([t, t], axis=0)
-                hi = f32(bf(a))
-                mid = f32(bf(a - hi))
-                first = jnp.where(low, hi, mid)
-                second = jnp.where(sub == 3, a - hi - mid, jnp.where(sub == 7, 1.0, first))
-                ypool[q * SB + i] = bf(jnp.concatenate([first, second], axis=0))
-                mom[q * SB + i] = jnp.zeros((8, BS), jnp.float32)
 
     def prepare(t, b):
         s = order[t]
@@ -380,11 +407,13 @@
                 out[g * 16 + j] = m[0:4] + m[4:8]
 
 
-def work(pidx, plan, vox, mass, low, own, high):
+def work(pidx, plan, vox, mass, ypool):
     moments = jax.ShapeDtypeStruct((SB, 4, BS), jnp.float32)
     scratch = [
         pltpu.VMEM((POOL, 8, BS), jnp.float32),
-        pltpu.VMEM((POOL, 16, BS), jnp.bfloat16),
+        pltpu.VMEM((3 * VB, BS), jnp.float32),
+        pltpu.VMEM((VB, BS), jnp.float32),
+        pltpu.SemaphoreType.DMA((2,)),
         pltpu.SMEM((VB + 8,), jnp.int32),
         pltpu.SMEM((VB + 8,), jnp.int32),
         pltpu.SMEM((N_GY,), jnp.int32),
@@ -398,23 +427,29 @@
     ] * (SLOTS * TOGETHER)
     return pl.pallas_call(
         work_kernel,
-        in_specs=[SMEM] * 2 + [VMEM] * 5,
+        in_specs=[SMEM] * 2 + [HBM] * 2 + [VMEM],
         out_specs=[VMEM] * 4,
         out_shape=[moments] * 3 + [jax.ShapeDtypeStruct((N_GY * GROUP, BS), jnp.float32)],
         scratch_shapes=scratch,
         compiler_params=pltpu.CompilerParams(vmem_limit_bytes=32 << 20),
         name="work",
-    )(pidx, plan, vox, mass, low, own, high)
+    )(
+        pidx,
+        plan,
+        pltpu.with_memory_space_constraint(vox, pltpu.HBM),
+        pltpu.with_memory_space_constraint(mass, pltpu.HBM),
+        ypool,
+    )
 
 
 def on_device(
     voxel_xyz, voxel_mass, candidates, offload_plan, seed_xyz, seed_pot, seed_target, seed_home
 ):
-    own_in, low_in, high_in, pidx = exchange(
+    ypool, pidx = exchange(
         jnp.transpose(seed_xyz, (1, 0, 2)), seed_pot, candidates.T, seed_home
     )
     vox = jnp.transpose(voxel_xyz, (1, 0, 2)).reshape(3 * VB, BS)
-    low, own, high, dual = work(pidx, offload_plan, vox, voxel_mass, low_in, own_in, high_in)
+    low, own, high, dual = work(pidx, offload_plan, vox, voxel_mass, ypool)
     flat = lambda m: m.reshape(4 * SB, BS)
     above_in, below_in, got = deliver(flat(low), flat(high), dual.reshape(N_GY, GROUP, BS))
     dual_pot, moments, new_pot = total(

time: 116 us -> 110 us (0.948)
  Pallas kernels: 114 us -> 108 us
    pallas_call x2, Pallas kernels: 80.7 us -> 35.8 us  [the longest x1 32.2 us: exchange(): pl.pallas_call(exchange_kernel, in_specs=[HBM] * 4, out_specs=[VMEM, SMEM...]
    pallas_call x1, Pallas kernels: 32 us -> 71 us  [deliver(): pl.pallas_call(deliver_kernel, in_specs=[VMEM] * 3, out_specs=[VMEM] * 3,...]
where the time goes in v5:
time: 110 us
  Pallas kernels  108 us (98%)
    pallas_call x1, Pallas kernels, deliver(): pl.pallas_call(deliver_kernel, in_specs=[VMEM] * 3, out_specs=[VMEM] * 3,...  71 us
    pallas_call x1, Pallas kernels, exchange(): pl.pallas_call(exchange_kernel, in_specs=[HBM] * 4, out_specs=[VMEM, SMEM...  32.2 us
    pallas_call x1, Pallas kernels, work(): pl.pallas_call(work_kernel, in_specs=[SMEM] * 2 + [HBM] * 2 + [VMEM], out...  3.6 us

profile of v5, /device:TPU:1, one launch (start us, length us, event | category | flops | bytes accessed | tf_op | source)
XLA Modules:
  0.0 109.5 jit_solution(15069413167690459594)
XLA Ops:
  0.6 0.0 copy-start
  0.6 0.0 copy-start.1
  0.7 32.2 %exchange.1 = (bf16[1536,16,128]{2,1,0:T(8,128)(2,1)S(1)}, s32[2048]{0:T(1024)S(1)}) custom-call(f32[3,512,128]{2,1,0:T(8,128)} %bitcast.14, f32[512,128]{1,0:T(8,128)} %pot.1, s32[8,256]{1,0:T(8,128)} %bitcast.16, s32[65536]{0:T(1024)} %home_hbm.1), custom_call_target="tpu_custom_call" | custom-call | tf_op jit(solution)/shard_map/exchange/pallas_call | solution.py:127
  32.8 0.0 copy-start.2
  32.8 0.7 copy-done.2
  33.5 3.6 %work.1 = (f32[512,4,128]{2,1,0:T(4,128)S(1)}, f32[512,4,128]{2,1,0:T(4,128)S(1)}, f32[512,4,128]{2,1,0:T(4,128)S(1)}, f32[320,128]{1,0:T(8,128)S(1)}) custom-call(s32[2048]{0:T(1024)S(1)} %get-tuple-element.15.pidx, s32[256]{0:T(256)S(1)} %copy-done.2, f32[768,128]{1,0:T(8,128)} %bitcast.15, f32[256,128]{1,0:T(8,128)} %mass_hbm.1, ...), custom_call_target="tpu_custom_call" | custom-call | tf_op jit(solution)/shard_map/work/pallas_call | solution.py:428
  37.1 71.0 %deliver.1 = (f32[2048,128]{1,0:T(8,128)S(1)}, f32[2048,128]{1,0:T(8,128)S(1)}, f32[8,40,128]{2,1,0:T(8,128)S(1)}) custom-call(f32[2048,128]{1,0:T(8,128)S(1)} %bitcast.10, f32[2048,128]{1,0:T(8,128)S(1)} %bitcast.11, f32[8,40,128]{2,1,0:T(8,128)S(1)} %bitcast.13), custom_call_target="tpu_custom_call" | custom-call | tf_op jit(solution)/shard_map/deliver/pallas_call | solution.py:187
  108.1 0.0 copy-done
  108.2 0.0 copy-done.1
  108.2 1.4 %total.1 = (f32[128,128]{1,0:T(8,128)}, f32[2048,128]{1,0:T(8,128)}, f32[512,128]{1,0:T(8,128)}) custom-call(f32[2048,128]{1,0:T(8,128)S(1)} %bitcast.12, f32[2048,128]{1,0:T(8,128)S(1)} %get-tuple-element.21.above_in, f32[2048,128]{1,0:T(8,128)S(1)} %get-tuple-element.22.below_in, f32[8,40,128]{2,1,0:T(8,128)S(1)} %get-tuple-element.23.got, ...), custom_call_target="tpu_custom_call" | custom-call | tf_op jit(solution)/shard_map/total/pallas_call | solution.py:254
Async XLA Ops:
  0.6 107.5 %copy-start = (f32[512,128]{1,0:T(8,128)S(1)}, f32[512,128]{1,0:T(8,128)}, u32[]{:S(2)}) copy-start(f32[512,128]{1,0:T(8,128)} %pot.1) | copy-start | bytes 786436
  0.6 107.5 %copy-start.1 = (f32[512,128]{1,0:T(8,128)S(1)}, f32[512,128]{1,0:T(8,128)}, u32[]{:S(2)}) copy-start(f32[512,128]{1,0:T(8,128)} %target.1) | copy-start | bytes 786436
  32.8 0.7 copy-start.2

commit v6 on v5

--- a/solution.py
+++ b/solution.py
@@ -18,7 +18,7 @@
 ROWS = 128
 GROUP = 40
 SLOTS = 4
-TOGETHER = 2
+TOGETHER = 4
 CHUNKS = 4
 
 EPS = 0.05
@@ -322,34 +322,39 @@
         b["xat"][...] = bf(xa.T)
         b["top"][0:1, :] = top
 
-    def weigh_and_spread(t, b, told, bold):
-        part = None
-        s = order[t] if t is not None else None
-        sold = order[told] if told is not None else None
+    def score(t, b, c):
+        s = order[t]
+        y = [ypool[pidx[s * KC + 2 * c + j]] for j in range(2)]
+        return jnp.dot(
+            b["xat"][...], jnp.concatenate(y, axis=1), preferred_element_type=jnp.float32
+        )
+
+    def spread(t, b, c):
+        s = order[t]
+        e = jnp.concatenate([b["split"][2 * c], b["split"][2 * c + 1]], axis=1)
+        m = jnp.dot(b["f8"][...], e, preferred_element_type=jnp.float32)
+        for j in range(2):
+            mom[pidx[s * KC + 2 * c + j]] += m[:, j * BS : (j + 1) * BS]
+
+    def weigh(sc, b, c, part):
+        e = jnp.exp2(sc)
+        eh = bf(e)
+        el = bf(e - f32(eh))
+        for j in range(2):
+            b["split"][2 * c + j, 0:BS, :] = eh[:, j * BS : (j + 1) * BS]
+            b["split"][2 * c + j, BS:, :] = el[:, j * BS : (j + 1) * BS]
+        p = e[:, :BS] + e[:, BS:]
+        return p if part is None else part + p
+
+    def weigh_and_spread(new, old):
+        parts = [None] * len(new)
         for c in range(KC // 2):
-            if t is not None:
-                y = [ypool[pidx[s * KC + 2 * c + j]] for j in range(2)]
-                sc = jnp.dot(
-                    b["xat"][...],
-                    jnp.concatenate(y, axis=1),
-                    preferred_element_type=jnp.float32,
-                )
-            if told is not None:
-                e2 = jnp.concatenate([bold["split"][2 * c], bold["split"][2 * c + 1]], axis=1)
-                m = jnp.dot(bold["f8"][...], e2, preferred_element_type=jnp.float32)
-                for j in range(2):
-                    mom[pidx[sold * KC + 2 * c + j]] += m[:, j * BS : (j + 1) * BS]
-            if t is not None:
-                e = jnp.exp2(sc)
-                eh = bf(e)
-                el = bf(e - f32(eh))
-                for j in range(2):
-                    b["split"][2 * c + j, 0:BS, :] = eh[:, j * BS : (j + 1) * BS]
-                    b["split"][2 * c + j, BS:, :] = el[:, j * BS : (j + 1) * BS]
-                p = e[:, :BS] + e[:, BS:]
-                part = p if part is None else part + p
-        if t is not None:
-            b["part"][...] = part
+            scores = [score(t, b, c) for t, b in new]
+            for t, b in old:
+                spread(t, b, c)
+            parts = [weigh(sc, b, c, p) for sc, (t, b), p in zip(scores, new, parts)]
+        for p, (t, b) in zip(parts, new):
+            b["part"][...] = p
 
     def norm(t, b):
         s = order[t]
@@ -372,16 +377,19 @@
         b["f8"][...] = jnp.concatenate([f8, f8], axis=1)
 
     def step(g, slot, valid):
-        for stage in range(3):
-            for u in range(TOGETHER):
-                at = lambda lag: (g - lag) * TOGETHER + u if valid(lag) else None
-                buf = lambda lag: bufs[((slot - lag) % SLOTS) * TOGETHER + u]
-                if stage == 0 and valid(0):
-                    prepare(at(0), buf(0))
-                if stage == 1 and (valid(1) or valid(3)):
-                    weigh_and_spread(at(1), buf(1), at(3), buf(3))
-                if stage == 2 and valid(2):
-                    norm(at(2), buf(2))
+        def blocks(lag):
+            if not valid(lag):
+                return []
+            first = ((slot - lag) % SLOTS) * TOGETHER
+            return [((g - lag) * TOGETHER + u, bufs[first + u]) for u in range(TOGETHER)]
+
+        for t, b in blocks(0):
+            prepare(t, b)
+        new, old = blocks(1), blocks(3)
+        for u in range(0, TOGETHER, 2):
+            weigh_and_spread(new[u : u + 2], old[u : u + 2])
+        for t, b in blocks(2):
+            norm(t, b)
 
     groups = n // TOGETHER
 

time: 110 us -> 107 us (0.973)
  Pallas kernels: 108 us -> 105 us
    pallas_call x1, Pallas kernels: 71 us -> 31.8 us  [deliver(): pl.pallas_call(deliver_kernel, in_specs=[VMEM] * 3, out_specs=[VMEM] * 3,...]
    pallas_call x1, Pallas kernels: 3.6 us -> 39.7 us  [work(): pl.pallas_call(work_kernel, in_specs=[SMEM] * 2 + [HBM] * 2 + [VMEM], out...]
where the time goes in v6:
time: 107 us; the launch traced here: 106 us
  Pallas kernels  105 us (98%)
    pallas_call x1, Pallas kernels, work(): pl.pallas_call(work_kernel, in_specs=[SMEM] * 2 + [HBM] * 2 + [VMEM], out...  39.7 us
    pallas_call x1, Pallas kernels, exchange(): pl.pallas_call(exchange_kernel, in_specs=[HBM] * 4, out_specs=[VMEM, SMEM...  32.2 us
    pallas_call x1, Pallas kernels, deliver(): pl.pallas_call(deliver_kernel, in_specs=[VMEM] * 3, out_specs=[VMEM] * 3,...  31.8 us

profile of v6, /device:TPU:1, one launch (start us, length us, event | category | flops | bytes accessed | tf_op | source)
XLA Modules:
  0.0 106.4 jit_solution(1200190646855176621)
XLA Ops:
  0.6 0.0 copy-start
  0.6 0.0 copy-start.1
  0.7 32.2 %exchange.1 = (bf16[1536,16,128]{2,1,0:T(8,128)(2,1)S(1)}, s32[2048]{0:T(1024)S(1)}) custom-call(f32[3,512,128]{2,1,0:T(8,128)} %bitcast.14, f32[512,128]{1,0:T(8,128)} %pot.1, s32[8,256]{1,0:T(8,128)} %bitcast.16, s32[65536]{0:T(1024)} %home_hbm.1), custom_call_target="tpu_custom_call" | custom-call | tf_op jit(solution)/shard_map/exchange/pallas_call | solution.py:127
  32.8 0.0 copy-start.2
  32.8 0.7 copy-done.2
  33.5 39.7 %work.1 = (f32[512,4,128]{2,1,0:T(4,128)S(1)}, f32[512,4,128]{2,1,0:T(4,128)S(1)}, f32[512,4,128]{2,1,0:T(4,128)S(1)}, f32[320,128]{1,0:T(8,128)S(1)}) custom-call(s32[2048]{0:T(1024)S(1)} %get-tuple-element.15.pidx, s32[256]{0:T(256)S(1)} %copy-done.2, f32[768,128]{1,0:T(8,128)} %bitcast.15, f32[256,128]{1,0:T(8,128)} %mass_hbm.1, ...), custom_call_target="tpu_custom_call" | custom-call | tf_op jit(solution)/shard_map/work/pallas_call | solution.py:436
  73.2 31.8 %deliver.1 = (f32[2048,128]{1,0:T(8,128)S(1)}, f32[2048,128]{1,0:T(8,128)S(1)}, f32[8,40,128]{2,1,0:T(8,128)S(1)}) custom-call(f32[2048,128]{1,0:T(8,128)S(1)} %bitcast.10, f32[2048,128]{1,0:T(8,128)S(1)} %bitcast.11, f32[8,40,128]{2,1,0:T(8,128)S(1)} %bitcast.13), custom_call_target="tpu_custom_call" | custom-call | tf_op jit(solution)/shard_map/deliver/pallas_call | solution.py:187
  105.0 0.0 copy-done
  105.0 0.0 copy-done.1
  105.1 1.4 %total.1 = (f32[128,128]{1,0:T(8,128)}, f32[2048,128]{1,0:T(8,128)}, f32[512,128]{1,0:T(8,128)}) custom-call(f32[2048,128]{1,0:T(8,128)S(1)} %bitcast.12, f32[2048,128]{1,0:T(8,128)S(1)} %get-tuple-element.21.above_in, f32[2048,128]{1,0:T(8,128)S(1)} %get-tuple-element.22.below_in, f32[8,40,128]{2,1,0:T(8,128)S(1)} %get-tuple-element.23.got, ...), custom_call_target="tpu_custom_call" | custom-call | tf_op jit(solution)/shard_map/total/pallas_call | solution.py:254
Async XLA Ops:
  0.6 104.4 %copy-start = (f32[512,128]{1,0:T(8,128)S(1)}, f32[512,128]{1,0:T(8,128)}, u32[]{:S(2)}) copy-start(f32[512,128]{1,0:T(8,128)} %pot.1) | copy-start | bytes 786436
  0.6 104.4 %copy-start.1 = (f32[512,128]{1,0:T(8,128)S(1)}, f32[512,128]{1,0:T(8,128)}, u32[]{:S(2)}) copy-start(f32[512,128]{1,0:T(8,128)} %target.1) | copy-start | bytes 786436
  32.8 0.7 copy-start.2

commit v7 on v6

--- a/solution.py
+++ b/solution.py
@@ -48,13 +48,14 @@
 
 
 def exchange_kernel(
-    xyz_hbm, pot_hbm, cand_hbm, home_hbm, ypool, pidx,
-    xyz, pot, plane, cand, home, load_sem, send_sem, recv_sem,
+    xyz_hbm, pot_hbm, cand_hbm, home_hbm, plan_hbm, ypool, pidx, listed,
+    xyz, pot, plane, cand, home, plan, load_sem, send_sem, recv_sem,
 ):
     x, g = lax.axis_index("gx"), lax.axis_index("gy")
     below, above = (x + N_GX - 1) % N_GX, (x + 1) % N_GX
     pairs = (
-        (xyz_hbm, xyz.at[1]), (pot_hbm, pot.at[1]), (cand_hbm, cand), (home_hbm, home)
+        (xyz_hbm, xyz.at[1]), (pot_hbm, pot.at[1]), (cand_hbm, cand), (home_hbm, home),
+        (plan_hbm, plan),
     )
     loads = [pltpu.make_async_copy(a, b, load_sem.at[i]) for i, (a, b) in enumerate(pairs)]
     for load in loads:
@@ -103,6 +104,35 @@
     loads[0].wait()
     loads[1].wait()
     build(1, 0, SB)
+    loads[4].wait()
+    p = jnp.concatenate([plan[0:1, :], plan[1:2, :]], axis=1)
+    wide = lambda axis, rows: lax.broadcasted_iota(jnp.int32, (rows, VB), axis)
+    taken = jnp.broadcast_to(p >= 0, (8, VB))
+    dest = jnp.broadcast_to((p >> 7) & 7, (8, VB))
+    one_hot = jnp.where(taken, jnp.where(dest == wide(0, 8), 1.0, 0.0), 0.0)
+    before = jnp.where(wide(0, VB) < wide(1, VB), 1.0, 0.0)
+    earlier = jnp.dot(bf(one_hot), bf(before), preferred_element_type=jnp.float32)
+    rank = jnp.sum(earlier * one_hot, axis=0, keepdims=True)
+    place = jnp.sum(earlier, axis=0, keepdims=True)
+    place = jnp.where(p >= 0, place, -1.0)
+    chosen = jnp.where(place == wide(0, VB).astype(jnp.float32), 1.0, 0.0)
+    facts = [
+        wide(1, 1).astype(jnp.float32),
+        ((p >> 7) & 7).astype(jnp.float32),
+        rank,
+        (p & 127).astype(jnp.float32),
+        jnp.zeros((4, VB), jnp.float32),
+    ]
+    facts = lax.dot_general(
+        bf(jnp.concatenate(facts, axis=0)),
+        bf(chosen),
+        (((1,), (1,)), ((), ())),
+        preferred_element_type=jnp.float32,
+    ).astype(jnp.int32)
+    count = jnp.sum(one_hot, axis=(0, 1), keepdims=True).astype(jnp.int32)
+    listed[0:1, :] = facts[0:1]
+    listed[1:2, :] = (facts[1:2] << 16) | (facts[2:3] << 8) | facts[3:4]
+    listed[2:8, :] = jnp.broadcast_to(count, (6, VB))
     loads[2].wait()
     loads[3].wait()
 
@@ -123,14 +153,15 @@
         copy.wait_send()
 
 
-def exchange(xyz, pot, cand, home):
+def exchange(xyz, pot, cand, home, plan):
     return pl.pallas_call(
         exchange_kernel,
-        in_specs=[HBM] * 4,
-        out_specs=[VMEM, SMEM],
+        in_specs=[HBM] * 5,
+        out_specs=[VMEM, SMEM, VMEM],
         out_shape=[
             jax.ShapeDtypeStruct((POOL, 16, BS), jnp.bfloat16),
             jax.ShapeDtypeStruct((VB * KC,), jnp.int32),
+            jax.ShapeDtypeStruct((8, VB), jnp.int32),
         ],
         scratch_shapes=[
             pltpu.VMEM((3, 3, SB, BS), jnp.float32),
@@ -138,7 +169,8 @@
             pltpu.VMEM((64, BS), jnp.float32),
             pltpu.SMEM((KC, VB), jnp.int32),
             pltpu.SMEM((N_GX * N_GY * SB,), jnp.int32),
-            pltpu.SemaphoreType.DMA((4,)),
+            pltpu.VMEM((VB // BS, BS), jnp.int32),
+            pltpu.SemaphoreType.DMA((5,)),
             pltpu.SemaphoreType.DMA((4 * CHUNKS,)),
             pltpu.SemaphoreType.DMA((4 * CHUNKS,)),
         ],
@@ -146,7 +178,7 @@
             collective_id=0, has_side_effects=True, vmem_limit_bytes=16 << 20
         ),
         name="exchange",
-    )(*(pltpu.with_memory_space_constraint(a, pltpu.HBM) for a in (xyz, pot, cand, home)))
+    )(*(pltpu.with_memory_space_constraint(a, pltpu.HBM) for a in (xyz, pot, cand, home, plan)))
 
 
 def deliver_kernel(
@@ -271,8 +303,8 @@
 
 
 def work_kernel(
-    pidx, plan, vox_hbm, mass_hbm, ypool,
-    low_out, own_out, high_out, dual, mom, vox, mass, sems, order, place, ranks, *scratch,
+    pidx, listed, vox_hbm, mass_hbm, ypool,
+    low_out, own_out, high_out, dual, mom, vox, mass, sems, *scratch,
 ):
     loads = [
         pltpu.make_async_copy(vox_hbm, vox, sems.at[0]),
@@ -281,25 +313,13 @@
     for load in loads:
         load.start()
     first_lane = (lax.axis_index("gy") & 3) * PAIR_CAP
-    for g in range(N_GY):
-        ranks[g] = 0
-
-    def compact(h, n):
-        for u in range(2):
-            v = 2 * h + u
-            p = plan[v]
-            occupied = (p >= 0).astype(jnp.int32)
-            dest = (p >> 7) & 7
-            rank = ranks[dest]
-            ranks[dest] = rank + occupied
-            order[n] = v
-            place[n] = (dest << 16) | (rank << 8) | (p & 127)
-            n = n + occupied
-            for j in range(POOL // VB):
-                mom[v * (POOL // VB) + j] = jnp.zeros((8, BS), jnp.float32)
-        return n
-
-    n = lax.fori_loop(0, VB // 2, compact, jnp.int32(0))
+    n = listed[2, 0]
+
+    @pl.loop(0, POOL // 16)
+    def _(i):
+        for j in range(16):
+            mom[i * 16 + j] = jnp.zeros((8, BS), jnp.float32)
+
     for load in loads:
         load.wait()
     size = len(BUFFERS)
@@ -308,7 +328,7 @@
     dual[...] = jnp.full(dual.shape, -1.0, jnp.float32)
 
     def prepare(t, b):
-        s = order[t]
+        s = listed[0, t]
         x = vox[pl.ds(s, 3, stride=VB), :] - 0.5
         xh = f32(bf(x))
         xl = x - xh
@@ -323,14 +343,14 @@
         b["top"][0:1, :] = top
 
     def score(t, b, c):
-        s = order[t]
+        s = listed[0, t]
         y = [ypool[pidx[s * KC + 2 * c + j]] for j in range(2)]
         return jnp.dot(
             b["xat"][...], jnp.concatenate(y, axis=1), preferred_element_type=jnp.float32
         )
 
     def spread(t, b, c):
-        s = order[t]
+        s = listed[0, t]
         e = jnp.concatenate([b["split"][2 * c], b["split"][2 * c + 1]], axis=1)
         m = jnp.dot(b["f8"][...], e, preferred_element_type=jnp.float32)
         for j in range(2):
@@ -357,12 +377,12 @@
             b["part"][...] = p
 
     def norm(t, b):
-        s = order[t]
+        s = listed[0, t]
         d = jnp.sum(b["part"][...].T, axis=0, keepdims=True)
         xr = vox[pl.ds(s, 3, stride=VB), :]
         x = xr - 0.5
         sq = jnp.sum(x * x, axis=0, keepdims=True)
-        where = place[t]
+        where = listed[1, t]
         top_row = (where >> 16) * GROUP
         rank = (where >> 8) & 255
         mark = pl.ds(top_row + PAIR_CAP, 1)
@@ -415,16 +435,13 @@
                 out[g * 16 + j] = m[0:4] + m[4:8]
 
 
-def work(pidx, plan, vox, mass, ypool):
+def work(pidx, listed, vox, mass, ypool):
     moments = jax.ShapeDtypeStruct((SB, 4, BS), jnp.float32)
     scratch = [
         pltpu.VMEM((POOL, 8, BS), jnp.float32),
         pltpu.VMEM((3 * VB, BS), jnp.float32),
         pltpu.VMEM((VB, BS), jnp.float32),
         pltpu.SemaphoreType.DMA((2,)),
-        pltpu.SMEM((VB + 8,), jnp.int32),
-        pltpu.SMEM((VB + 8,), jnp.int32),
-        pltpu.SMEM((N_GY,), jnp.int32),
     ]
     scratch += [
         pltpu.VMEM((KC, 2 * BS, BS), jnp.bfloat16),
@@ -443,7 +460,7 @@
         name="work",
     )(
         pidx,
-        plan,
+        listed,
         pltpu.with_memory_space_constraint(vox, pltpu.HBM),
         pltpu.with_memory_space_constraint(mass, pltpu.HBM),
         ypool,
@@ -453,11 +470,15 @@
 def on_device(
     voxel_xyz, voxel_mass, candidates, offload_plan, seed_xyz, seed_pot, seed_target, seed_home
 ):
-    ypool, pidx = exchange(
-        jnp.transpose(seed_xyz, (1, 0, 2)), seed_pot, candidates.T, seed_home
+    ypool, pidx, listed = exchange(
+        jnp.transpose(seed_xyz, (1, 0, 2)),
+        seed_pot,
+        candidates.T,
+        seed_home,
+        offload_plan.reshape(VB // BS, BS),
     )
     vox = jnp.transpose(voxel_xyz, (1, 0, 2)).reshape(3 * VB, BS)
-    low, own, high, dual = work(pidx, offload_plan, vox, voxel_mass, ypool)
+    low, own, high, dual = work(pidx, listed, vox, voxel_mass, ypool)
     flat = lambda m: m.reshape(4 * SB, BS)
     above_in, below_in, got = deliver(flat(low), flat(high), dual.reshape(N_GY, GROUP, BS))
     dual_pot, moments, new_pot = total(

time: 107 us -> 104 us (0.972)
    pallas_call x1, Pallas kernels: 39.7 us -> 2.77 us  [work(): pl.pallas_call(work_kernel, in_specs=[SMEM] * 2 + [HBM] * 2 + [VMEM], out...]
    pallas_call x1, Pallas kernels: 31.8 us -> 67.2 us  [deliver(): pl.pallas_call(deliver_kernel, in_specs=[VMEM] * 3, out_specs=[VMEM] * 3,...]
where the time goes in v7:
time: 104 us
  Pallas kernels  104 us (100%)
    pallas_call x1, Pallas kernels, deliver(): pl.pallas_call(deliver_kernel, in_specs=[VMEM] * 3, out_specs=[VMEM] * 3,...  67.2 us
    pallas_call x1, Pallas kernels, exchange(): pl.pallas_call(exchange_kernel, in_specs=[HBM] * 5, out_specs=[VMEM, SMEM...  32.2 us
    pallas_call x1, Pallas kernels, work(): pl.pallas_call(work_kernel, in_specs=[SMEM] * 2 + [HBM] * 2 + [VMEM], out...  2.77 us

profile of v7, /device:TPU:1, one launch (start us, length us, event | category | flops | bytes accessed | tf_op | source)
XLA Modules:
  0.0 104.2 jit_solution(17416848477078414234)
XLA Ops:
  0.6 0.0 copy-start
  0.6 0.0 copy-start.1
  0.7 32.2 %exchange.1 = (bf16[1536,16,128]{2,1,0:T(8,128)(2,1)S(1)}, s32[2048]{0:T(1024)S(1)}, s32[8,256]{1,0:T(8,128)S(1)}) custom-call(f32[3,512,128]{2,1,0:T(8,128)} %bitcast.15, f32[512,128]{1,0:T(8,128)} %pot.1, s32[8,256]{1,0:T(8,128)} %bitcast.17, s32[65536]{0:T(1024)} %home_hbm.1, s32[2,128]{1,0:T(2,128)} %bitcast.18), custom_call_target="tpu_custom_call" | custom-call | tf_op jit(solution)/shard_map/exchange/pallas_call | solution.py:157
  32.8 2.8 %work.1 = (f32[512,4,128]{2,1,0:T(4,128)S(1)}, f32[512,4,128]{2,1,0:T(4,128)S(1)}, f32[512,4,128]{2,1,0:T(4,128)S(1)}, f32[320,128]{1,0:T(8,128)S(1)}) custom-call(s32[2048]{0:T(1024)S(1)} %get-tuple-element.16.pidx, s32[8,256]{1,0:T(8,128)S(1)} %get-tuple-element.17.listed, f32[768,128]{1,0:T(8,128)} %bitcast.16, f32[256,128]{1,0:T(8,128)} %mass_hbm.1, ...), custom_call_target="tpu_custom_call" | custom-call | tf_op jit(solution)/shard_map/work/pallas_call | solution.py:453
  35.6 67.2 %deliver.1 = (f32[2048,128]{1,0:T(8,128)S(1)}, f32[2048,128]{1,0:T(8,128)S(1)}, f32[8,40,128]{2,1,0:T(8,128)S(1)}) custom-call(f32[2048,128]{1,0:T(8,128)S(1)} %bitcast.11, f32[2048,128]{1,0:T(8,128)S(1)} %bitcast.12, f32[8,40,128]{2,1,0:T(8,128)S(1)} %bitcast.14), custom_call_target="tpu_custom_call" | custom-call | tf_op jit(solution)/shard_map/deliver/pallas_call | solution.py:219
  102.8 0.0 copy-done
  102.8 0.0 copy-done.1
  102.9 1.4 %total.1 = (f32[128,128]{1,0:T(8,128)}, f32[2048,128]{1,0:T(8,128)}, f32[512,128]{1,0:T(8,128)}) custom-call(f32[2048,128]{1,0:T(8,128)S(1)} %bitcast.13, f32[2048,128]{1,0:T(8,128)S(1)} %get-tuple-element.23.above_in, f32[2048,128]{1,0:T(8,128)S(1)} %get-tuple-element.24.below_in, f32[8,40,128]{2,1,0:T(8,128)S(1)} %get-tuple-element.25.got, ...), custom_call_target="tpu_custom_call" | custom-call | tf_op jit(solution)/shard_map/total/pallas_call | solution.py:286
Async XLA Ops:
  0.6 102.2 %copy-start = (f32[512,128]{1,0:T(8,128)S(1)}, f32[512,128]{1,0:T(8,128)}, u32[]{:S(2)}) copy-start(f32[512,128]{1,0:T(8,128)} %pot.1) | copy-start | bytes 786436
  0.6 102.2 %copy-start.1 = (f32[512,128]{1,0:T(8,128)S(1)}, f32[512,128]{1,0:T(8,128)}, u32[]{:S(2)}) copy-start(f32[512,128]{1,0:T(8,128)} %target.1) | copy-start | bytes 786436

commit v8 on v7

--- a/solution.py
+++ b/solution.py
@@ -48,14 +48,14 @@
 
 
 def exchange_kernel(
-    xyz_hbm, pot_hbm, cand_hbm, home_hbm, plan_hbm, ypool, pidx, listed,
-    xyz, pot, plane, cand, home, plan, load_sem, send_sem, recv_sem,
+    xyz_hbm, pot_hbm, cand_hbm, home_hbm, plan_hbm, vox_hbm, ypool, tops, xats, pidx, listed,
+    xyz, pot, plane, cand, home, plan, vox, load_sem, send_sem, recv_sem,
 ):
     x, g = lax.axis_index("gx"), lax.axis_index("gy")
     below, above = (x + N_GX - 1) % N_GX, (x + 1) % N_GX
     pairs = (
         (xyz_hbm, xyz.at[1]), (pot_hbm, pot.at[1]), (cand_hbm, cand), (home_hbm, home),
-        (plan_hbm, plan),
+        (plan_hbm, plan), (vox_hbm, vox),
     )
     loads = [pltpu.make_async_copy(a, b, load_sem.at[i]) for i, (a, b) in enumerate(pairs)]
     for load in loads:
@@ -91,20 +91,36 @@
                 y = xyz[slot, c, pl.ds(at, 16), :] - 0.5
                 plane[c * 16 : (c + 1) * 16, :] = (2.0 * LOG2E / EPS) * y
                 square = y * y if square is None else square + y * y
-            plane[48:64, :] = LOG2E * (pot[slot, pl.ds(at, 16), :] - (1.0 / EPS) * square)
+            offset = LOG2E * (pot[slot, pl.ds(at, 16), :] - (1.0 / EPS) * square)
+            plane[48:64, :] = offset
+            top = f32(bf(jnp.max(offset, axis=1, keepdims=True)))
+            tops[pl.ds(slot * SB + at, 16), :] = jnp.broadcast_to(top, (16, BS))
             for j in range(16):
                 t = plane[pl.ds(j, 4, stride=16), :]
                 a = jnp.concatenate([t, t], axis=0)
                 hi = f32(bf(a))
                 mid = f32(bf(a - hi))
                 first = jnp.where(low, hi, mid)
-                second = jnp.where(sub == 3, a - hi - mid, jnp.where(sub == 7, 1.0, first))
+                second = jnp.where(sub == 3, a - hi - mid, jnp.where(sub == 7, 0.0, first))
                 ypool[slot * SB + at + j] = bf(jnp.concatenate([first, second], axis=0))
 
     loads[0].wait()
     loads[1].wait()
     build(1, 0, SB)
     loads[4].wait()
+    loads[5].wait()
+
+    @pl.loop(0, VB // 4)
+    def _(h):
+        for u in range(4):
+            v = h * 4 + u
+            x = vox[pl.ds(v, 3, stride=VB), :] - 0.5
+            xh = f32(bf(x))
+            xl = x - xh
+            one = jnp.ones((1, BS), jnp.float32)
+            xa = jnp.concatenate([xh, one, xh, one, xl, one, xl, one], axis=0)
+            xats[v] = bf(xa.T)
+
     p = jnp.concatenate([plan[0:1, :], plan[1:2, :]], axis=1)
     wide = lambda axis, rows: lax.broadcasted_iota(jnp.int32, (rows, VB), axis)
     taken = jnp.broadcast_to(p >= 0, (8, VB))
@@ -153,13 +169,15 @@
         copy.wait_send()
 
 
-def exchange(xyz, pot, cand, home, plan):
+def exchange(xyz, pot, cand, home, plan, vox):
     return pl.pallas_call(
         exchange_kernel,
-        in_specs=[HBM] * 5,
-        out_specs=[VMEM, SMEM, VMEM],
+        in_specs=[HBM] * 6,
+        out_specs=[VMEM, VMEM, VMEM, SMEM, VMEM],
         out_shape=[
             jax.ShapeDtypeStruct((POOL, 16, BS), jnp.bfloat16),
+            jax.ShapeDtypeStruct((POOL, BS), jnp.float32),
+            jax.ShapeDtypeStruct((VB, BS, 16), jnp.bfloat16),
             jax.ShapeDtypeStruct((VB * KC,), jnp.int32),
             jax.ShapeDtypeStruct((8, VB), jnp.int32),
         ],
@@ -170,15 +188,16 @@
             pltpu.SMEM((KC, VB), jnp.int32),
             pltpu.SMEM((N_GX * N_GY * SB,), jnp.int32),
             pltpu.VMEM((VB // BS, BS), jnp.int32),
-            pltpu.SemaphoreType.DMA((5,)),
+            pltpu.VMEM((3 * VB, BS), jnp.float32),
+            pltpu.SemaphoreType.DMA((6,)),
             pltpu.SemaphoreType.DMA((4 * CHUNKS,)),
             pltpu.SemaphoreType.DMA((4 * CHUNKS,)),
         ],
         compiler_params=pltpu.CompilerParams(
-            collective_id=0, has_side_effects=True, vmem_limit_bytes=16 << 20
+            collective_id=0, has_side_effects=True, vmem_limit_bytes=24 << 20
         ),
         name="exchange",
-    )(*(pltpu.with_memory_space_constraint(a, pltpu.HBM) for a in (xyz, pot, cand, home, plan)))
+    )(*(pltpu.with_memory_space_constraint(a, pltpu.HBM) for a in (xyz, pot, cand, home, plan, vox)))
 
 
 def deliver_kernel(
@@ -299,11 +318,11 @@
     )(own, above_in, below_in, got, pot, target)
 
 
-BUFFERS = ("split", "xat", "part", "top", "f8")
+BUFFERS = ("split", "shift", "part", "top", "f8")
 
 
 def work_kernel(
-    pidx, listed, vox_hbm, mass_hbm, ypool,
+    pidx, listed, vox_hbm, mass_hbm, ypool, tops, xats,
     low_out, own_out, high_out, dual, mom, vox, mass, sems, *scratch,
 ):
     loads = [
@@ -327,26 +346,21 @@
     lane = lax.broadcasted_iota(jnp.int32, (1, BS), 1)
     dual[...] = jnp.full(dual.shape, -1.0, jnp.float32)
 
+    last = lax.broadcasted_iota(jnp.int32, (16, BS), 0) == 15
+
     def prepare(t, b):
         s = listed[0, t]
-        x = vox[pl.ds(s, 3, stride=VB), :] - 0.5
-        xh = f32(bf(x))
-        xl = x - xh
-        tops = [f32(ypool[pidx[s * KC + k], 0:8, :]) for k in range(KC)]
-        while len(tops) > 1:
-            tops = [jnp.maximum(a, c) for a, c in zip(tops[::2], tops[1::2])]
-        top = jnp.max(tops[0][3:4], axis=1, keepdims=True)
-        top = jnp.broadcast_to(top, (1, BS))
-        one = jnp.ones((1, BS), jnp.float32)
-        xa = jnp.concatenate([xh, one, xh, one, xl, one, xl, -top], axis=0)
-        b["xat"][...] = bf(xa.T)
-        b["top"][0:1, :] = top
+        high = [tops[pl.ds(pidx[s * KC + k], 1), :] for k in range(KC)]
+        while len(high) > 1:
+            high = [jnp.maximum(a, c) for a, c in zip(high[::2], high[1::2])]
+        b["top"][0:1, :] = high[0]
+        b["shift"][...] = bf(jnp.where(last, -high[0], 0.0))
 
     def score(t, b, c):
         s = listed[0, t]
-        y = [ypool[pidx[s * KC + 2 * c + j]] for j in range(2)]
+        y = [ypool[pidx[s * KC + 2 * c + j]] + b["shift"][...] for j in range(2)]
         return jnp.dot(
-            b["xat"][...], jnp.concatenate(y, axis=1), preferred_element_type=jnp.float32
+            xats[s], jnp.concatenate(y, axis=1), preferred_element_type=jnp.float32
         )
 
     def spread(t, b, c):
@@ -435,7 +449,7 @@
                 out[g * 16 + j] = m[0:4] + m[4:8]
 
 
-def work(pidx, listed, vox, mass, ypool):
+def work(pidx, listed, vox, mass, ypool, tops, xats):
     moments = jax.ShapeDtypeStruct((SB, 4, BS), jnp.float32)
     scratch = [
         pltpu.VMEM((POOL, 8, BS), jnp.float32),
@@ -445,14 +459,14 @@
     ]
     scratch += [
         pltpu.VMEM((KC, 2 * BS, BS), jnp.bfloat16),
-        pltpu.VMEM((BS, 16), jnp.bfloat16),
+        pltpu.VMEM((16, BS), jnp.bfloat16),
         pltpu.VMEM((BS, BS), jnp.float32),
         pltpu.VMEM((8, BS), jnp.float32),
         pltpu.VMEM((8, 2 * BS), jnp.bfloat16),
     ] * (SLOTS * TOGETHER)
     return pl.pallas_call(
         work_kernel,
-        in_specs=[SMEM] * 2 + [HBM] * 2 + [VMEM],
+        in_specs=[SMEM] * 2 + [HBM] * 2 + [VMEM] * 3,
         out_specs=[VMEM] * 4,
         out_shape=[moments] * 3 + [jax.ShapeDtypeStruct((N_GY * GROUP, BS), jnp.float32)],
         scratch_shapes=scratch,
@@ -464,21 +478,24 @@
         pltpu.with_memory_space_constraint(vox, pltpu.HBM),
         pltpu.with_memory_space_constraint(mass, pltpu.HBM),
         ypool,
+        tops,
+        xats,
     )
 
 
 def on_device(
     voxel_xyz, voxel_mass, candidates, offload_plan, seed_xyz, seed_pot, seed_target, seed_home
 ):
-    ypool, pidx, listed = exchange(
+    vox = jnp.transpose(voxel_xyz, (1, 0, 2)).reshape(3 * VB, BS)
+    ypool, tops, xats, pidx, listed = exchange(
         jnp.transpose(seed_xyz, (1, 0, 2)),
         seed_pot,
         candidates.T,
         seed_home,
         offload_plan.reshape(VB // BS, BS),
+        vox,
     )
-    vox = jnp.transpose(voxel_xyz, (1, 0, 2)).reshape(3 * VB, BS)
-    low, own, high, dual = work(pidx, listed, vox, voxel_mass, ypool)
+    low, own, high, dual = work(pidx, listed, vox, voxel_mass, ypool, tops, xats)
     flat = lambda m: m.reshape(4 * SB, BS)
     above_in, below_in, got = deliver(flat(low), flat(high), dual.reshape(N_GY, GROUP, BS))
     dual_pot, moments, new_pot = total(

time: 104 us -> 108 us (1.038)
  Pallas kernels: 104 us -> 107 us
    pallas_call x2, Pallas kernels: 35 us -> 73.3 us  [the longest x1 40.5 us: work(): pl.pallas_call(work_kernel, in_specs=[SMEM] * 2 + [HBM] * 2 + [VMEM] * 3,...]
    pallas_call x1, Pallas kernels: 67.2 us -> 32.1 us  [deliver(): pl.pallas_call(deliver_kernel, in_specs=[VMEM] * 3, out_specs=[VMEM] * 3,...]
where the time goes in v8:
time: 108 us; the launch traced here: 107 us
  Pallas kernels  107 us (99%)
    pallas_call x1, Pallas kernels, work(): pl.pallas_call(work_kernel, in_specs=[SMEM] * 2 + [HBM] * 2 + [VMEM] * 3,...  40.5 us
    pallas_call x1, Pallas kernels, exchange(): pl.pallas_call(exchange_kernel, in_specs=[HBM] * 6, out_specs=[VMEM, VMEM...  32.8 us
    pallas_call x1, Pallas kernels, deliver(): pl.pallas_call(deliver_kernel, in_specs=[VMEM] * 3, out_specs=[VMEM] * 3,...  32.1 us

profile of v8, /device:TPU:1, one launch (start us, length us, event | category | flops | bytes accessed | tf_op | source)
XLA Modules:
  0.0 107.5 jit_solution(14013244237210419114)
XLA Ops:
  0.6 32.8 %exchange.1 = (bf16[1536,16,128]{2,1,0:T(8,128)(2,1)S(1)}, f32[1536,128]{1,0:T(8,128)S(1)}, bf16[256,128,16]{2,1,0:T(8,128)(2,1)S(1)}, s32[2048]{0:T(1024)S(1)}, s32[8,256]{1,0:T(8,128)S(1)}) custom-call(f32[3,512,128]{2,1,0:T(8,128)} %bitcast.17, f32[512,128]{1,0:T(8,128)} %pot.1, s32[8,256]{1,0:T(8,128)} %bitcast.18, s32[65536]{0:T(1024)} %home_hbm.1, ...), custom_call_target="tpu_custom_call" | custom-call | tf_op jit(solution)/shard_map/exchange/pallas_call | solution.py:173
  33.5 0.0 copy-start
  33.5 0.0 copy-start.1
  33.5 40.5 %work.1 = (f32[512,4,128]{2,1,0:T(4,128)S(1)}, f32[512,4,128]{2,1,0:T(4,128)S(1)}, f32[512,4,128]{2,1,0:T(4,128)S(1)}, f32[320,128]{1,0:T(8,128)S(1)}) custom-call(s32[2048]{0:T(1024)S(1)} %get-tuple-element.18.pidx, s32[8,256]{1,0:T(8,128)S(1)} %get-tuple-element.19.listed, f32[768,128]{1,0:T(8,128)} %bitcast.16, f32[256,128]{1,0:T(8,128)} %mass_hbm.1, ...), custom_call_target="tpu_custom_call" | custom-call | tf_op jit(solution)/shard_map/work/pallas_call | solution.py:467
  74.0 32.1 %deliver.1 = (f32[2048,128]{1,0:T(8,128)S(1)}, f32[2048,128]{1,0:T(8,128)S(1)}, f32[8,40,128]{2,1,0:T(8,128)S(1)}) custom-call(f32[2048,128]{1,0:T(8,128)S(1)} %bitcast.11, f32[2048,128]{1,0:T(8,128)S(1)} %bitcast.12, f32[8,40,128]{2,1,0:T(8,128)S(1)} %bitcast.14), custom_call_target="tpu_custom_call" | custom-call | tf_op jit(solution)/shard_map/deliver/pallas_call | solution.py:238
  106.1 0.0 copy-done
  106.1 0.0 copy-done.1
  106.1 1.4 %total.1 = (f32[128,128]{1,0:T(8,128)}, f32[2048,128]{1,0:T(8,128)}, f32[512,128]{1,0:T(8,128)}) custom-call(f32[2048,128]{1,0:T(8,128)S(1)} %bitcast.13, f32[2048,128]{1,0:T(8,128)S(1)} %get-tuple-element.27.above_in, f32[2048,128]{1,0:T(8,128)S(1)} %get-tuple-element.28.below_in, f32[8,40,128]{2,1,0:T(8,128)S(1)} %get-tuple-element.29.got, ...), custom_call_target="tpu_custom_call" | custom-call | tf_op jit(solution)/shard_map/total/pallas_call | solution.py:305
Async XLA Ops:
  33.5 72.6 %copy-start = (f32[512,128]{1,0:T(8,128)S(1)}, f32[512,128]{1,0:T(8,128)}, u32[]{:S(2)}) copy-start(f32[512,128]{1,0:T(8,128)} %pot.1) | copy-start | bytes 786436
  33.5 72.6 %copy-start.1 = (f32[512,128]{1,0:T(8,128)S(1)}, f32[512,128]{1,0:T(8,128)}, u32[]{:S(2)}) copy-start(f32[512,128]{1,0:T(8,128)} %target.1) | copy-start | bytes 786436

commit v9 on v7

--- a/solution.py
+++ b/solution.py
@@ -19,7 +19,7 @@
 GROUP = 40
 SLOTS = 4
 TOGETHER = 4
-CHUNKS = 4
+CHUNKS = 8
 
 EPS = 0.05
 STEP = 0.5
@@ -182,7 +182,8 @@
 
 
 def deliver_kernel(
-    low, high, dual, above_in, below_in, got, dual_send, dual_recv, send_sem, recv_sem, own_sem
+    low, high, dual, above_in, below_in, dual_pot,
+    got, dual_send, dual_recv, send_sem, recv_sem, own_sem,
 ):
     x, g = lax.axis_index("gx"), lax.axis_index("gy")
     below, above = (x + N_GX - 1) % N_GX, (x + 1) % N_GX
@@ -210,56 +211,8 @@
         copy.start()
     keep.start()
     keep.wait()
-    for copy in copies:
+    for copy in copies[2:]:
         copy.wait()
-
-
-def deliver(low, high, dual):
-    moments = jax.ShapeDtypeStruct((4 * SB, BS), jnp.float32)
-    return pl.pallas_call(
-        deliver_kernel,
-        in_specs=[VMEM] * 3,
-        out_specs=[VMEM] * 3,
-        out_shape=[moments] * 2 + [jax.ShapeDtypeStruct((N_GY, GROUP, BS), jnp.float32)],
-        scratch_shapes=[
-            pltpu.SemaphoreType.DMA((N_GY - 1,)),
-            pltpu.SemaphoreType.DMA((N_GY - 1,)),
-            pltpu.SemaphoreType.DMA((2,)),
-            pltpu.SemaphoreType.DMA((2,)),
-            pltpu.SemaphoreType.DMA(()),
-        ],
-        compiler_params=pltpu.CompilerParams(
-            collective_id=1, has_side_effects=True, vmem_limit_bytes=16 << 20
-        ),
-        name="deliver",
-    )(low, high, dual)
-
-
-def total_kernel(
-    own, above_in, below_in, got, pot, target, dual_hbm, moments_hbm, new_pot_hbm,
-    moments, new_pot, dual_pot, sems,
-):
-    parts = 4
-    size = 4 * SB // parts
-    sends = []
-    for q in range(parts):
-
-        @pl.loop(0, SB // 16 // parts)
-        def _(i):
-            at = pl.multiple_of(q * size + i * 64, 64)
-            moments[pl.ds(at, 64), :] = (
-                own[pl.ds(at, 64), :] + above_in[pl.ds(at, 64), :] + below_in[pl.ds(at, 64), :]
-            )
-            for j in range(2):
-                rows = pl.ds(pl.multiple_of(q * (size // 4) + i * 16, 16) + 8 * j, 8)
-                mass = moments[pl.ds(at + 32 * j, 8, stride=4), :]
-                new_pot[rows, :] = pot[rows, :] + STEP * (target[rows, :] - mass)
-
-        some = pl.ds(q * size, size)
-        sends.append(pltpu.make_async_copy(moments.at[some], moments_hbm.at[some], sems.at[q]))
-        sends[-1].start()
-    sends.append(pltpu.make_async_copy(new_pot, new_pot_hbm, sems.at[parts]))
-    sends[-1].start()
     row = lax.broadcasted_iota(jnp.int32, (ROWS, BS), 0).astype(jnp.float32)
     total = None
     for half in range(2):
@@ -275,13 +228,63 @@
             term = jnp.dot(hot, piece, preferred_element_type=jnp.float32)
             total = term if total is None else total + term
     dual_pot[...] = total
-    sends.append(pltpu.make_async_copy(dual_pot, dual_hbm, sems.at[parts + 1]))
+    for copy in copies[:2]:
+        copy.wait()
+
+
+def deliver(low, high, dual):
+    moments = jax.ShapeDtypeStruct((4 * SB, BS), jnp.float32)
+    return pl.pallas_call(
+        deliver_kernel,
+        in_specs=[VMEM] * 3,
+        out_specs=[VMEM] * 3,
+        out_shape=[moments] * 2 + [jax.ShapeDtypeStruct((ROWS, BS), jnp.float32)],
+        scratch_shapes=[
+            pltpu.VMEM((N_GY, GROUP, BS), jnp.float32),
+            pltpu.SemaphoreType.DMA((N_GY - 1,)),
+            pltpu.SemaphoreType.DMA((N_GY - 1,)),
+            pltpu.SemaphoreType.DMA((2,)),
+            pltpu.SemaphoreType.DMA((2,)),
+            pltpu.SemaphoreType.DMA(()),
+        ],
+        compiler_params=pltpu.CompilerParams(
+            collective_id=1, has_side_effects=True, vmem_limit_bytes=16 << 20
+        ),
+        name="deliver",
+    )(low, high, dual)
+
+
+def total_kernel(
+    own, above_in, below_in, dual_pot, pot, target, dual_hbm, moments_hbm, new_pot_hbm,
+    moments, new_pot, sems,
+):
+    parts = 4
+    size = 4 * SB // parts
+    sends = [pltpu.make_async_copy(dual_pot, dual_hbm, sems.at[parts + 1])]
+    sends[0].start()
+    for q in range(parts):
+
+        @pl.loop(0, SB // 16 // parts)
+        def _(i):
+            at = pl.multiple_of(q * size + i * 64, 64)
+            moments[pl.ds(at, 64), :] = (
+                own[pl.ds(at, 64), :] + above_in[pl.ds(at, 64), :] + below_in[pl.ds(at, 64), :]
+            )
+            for j in range(2):
+                rows = pl.ds(pl.multiple_of(q * (size // 4) + i * 16, 16) + 8 * j, 8)
+                mass = moments[pl.ds(at + 32 * j, 8, stride=4), :]
+                new_pot[rows, :] = pot[rows, :] + STEP * (target[rows, :] - mass)
+
+        some = pl.ds(q * size, size)
+        sends.append(pltpu.make_async_copy(moments.at[some], moments_hbm.at[some], sems.at[q]))
+        sends[-1].start()
+    sends.append(pltpu.make_async_copy(new_pot, new_pot_hbm, sems.at[parts]))
     sends[-1].start()
     for send in sends:
         send.wait()
 
 
-def total(own, above_in, below_in, got, pot, target):
+def total(own, above_in, below_in, dual_pot, pot, target):
     shapes = [(ROWS, BS), (4 * SB, BS), (SB, BS)]
     return pl.pallas_call(
         total_kernel,
@@ -291,12 +294,11 @@
         scratch_shapes=[
             pltpu.VMEM((4 * SB, BS), jnp.float32),
             pltpu.VMEM((SB, BS), jnp.float32),
-            pltpu.VMEM((ROWS, BS), jnp.float32),
             pltpu.SemaphoreType.DMA((6,)),
         ],
         compiler_params=pltpu.CompilerParams(vmem_limit_bytes=16 << 20),
         name="total",
-    )(own, above_in, below_in, got, pot, target)
+    )(own, above_in, below_in, dual_pot, pot, target)
 
 
 BUFFERS = ("split", "xat", "part", "top", "f8")
@@ -403,11 +405,11 @@
             first = ((slot - lag) % SLOTS) * TOGETHER
             return [((g - lag) * TOGETHER + u, bufs[first + u]) for u in range(TOGETHER)]
 
-        for t, b in blocks(0):
-            prepare(t, b)
         new, old = blocks(1), blocks(3)
         for u in range(0, TOGETHER, 2):
             weigh_and_spread(new[u : u + 2], old[u : u + 2])
+        for t, b in blocks(0):
+            prepare(t, b)
         for t, b in blocks(2):
             norm(t, b)
 
@@ -480,9 +482,9 @@
     vox = jnp.transpose(voxel_xyz, (1, 0, 2)).reshape(3 * VB, BS)
     low, own, high, dual = work(pidx, listed, vox, voxel_mass, ypool)
     flat = lambda m: m.reshape(4 * SB, BS)
-    above_in, below_in, got = deliver(flat(low), flat(high), dual.reshape(N_GY, GROUP, BS))
+    above_in, below_in, placed = deliver(flat(low), flat(high), dual.reshape(N_GY, GROUP, BS))
     dual_pot, moments, new_pot = total(
-        flat(own), above_in, below_in, got, seed_pot, seed_target
+        flat(own), above_in, below_in, placed, seed_pot, seed_target
     )
     return (dual_pot, moments.reshape(SB, 4, BS), new_pot)
 

time: 104 us -> 105 us (level)
    pallas_call x1, Pallas kernels: 2.77 us -> 39.4 us  [work(): pl.pallas_call(work_kernel, in_specs=[SMEM] * 2 + [HBM] * 2 + [VMEM], out...]
    pallas_call x1, Pallas kernels: 67.2 us -> 32.1 us  [deliver(): pl.pallas_call(deliver_kernel, in_specs=[VMEM] * 3, out_specs=[VMEM] * 3,...]
where the time goes in v9:
time: 105 us; the launch traced here: 106 us
  Pallas kernels  105 us (100%)
    pallas_call x1, Pallas kernels, work(): pl.pallas_call(work_kernel, in_specs=[SMEM] * 2 + [HBM] * 2 + [VMEM], out...  39.4 us
    pallas_call x1, Pallas kernels, deliver(): pl.pallas_call(deliver_kernel, in_specs=[VMEM] * 3, out_specs=[VMEM] * 3,...  32.1 us
    pallas_call x1, Pallas kernels, exchange(): pl.pallas_call(exchange_kernel, in_specs=[HBM] * 5, out_specs=[VMEM, SMEM...  32.1 us

profile of v9, /device:TPU:1, one launch (start us, length us, event | category | flops | bytes accessed | tf_op | source)
XLA Modules:
  0.0 105.7 jit_solution(2460167257555378958)
XLA Ops:
  0.6 0.0 copy-start
  0.6 0.0 copy-start.1
  0.7 32.1 %exchange.1 = (bf16[1536,16,128]{2,1,0:T(8,128)(2,1)S(1)}, s32[2048]{0:T(1024)S(1)}, s32[8,256]{1,0:T(8,128)S(1)}) custom-call(f32[3,512,128]{2,1,0:T(8,128)} %bitcast.15, f32[512,128]{1,0:T(8,128)} %pot.1, s32[8,256]{1,0:T(8,128)} %bitcast.17, s32[65536]{0:T(1024)} %home_hbm.1, s32[2,128]{1,0:T(2,128)} %bitcast.18), custom_call_target="tpu_custom_call" | custom-call | tf_op jit(solution)/shard_map/exchange/pallas_call | solution.py:157
  32.8 39.4 %work.1 = (f32[512,4,128]{2,1,0:T(4,128)S(1)}, f32[512,4,128]{2,1,0:T(4,128)S(1)}, f32[512,4,128]{2,1,0:T(4,128)S(1)}, f32[320,128]{1,0:T(8,128)S(1)}) custom-call(s32[2048]{0:T(1024)S(1)} %get-tuple-element.16.pidx, s32[8,256]{1,0:T(8,128)S(1)} %get-tuple-element.17.listed, f32[768,128]{1,0:T(8,128)} %bitcast.16, f32[256,128]{1,0:T(8,128)} %mass_hbm.1, ...), custom_call_target="tpu_custom_call" | custom-call | tf_op jit(solution)/shard_map/work/pallas_call | solution.py:455
  72.2 32.1 %deliver.1 = (f32[2048,128]{1,0:T(8,128)S(1)}, f32[2048,128]{1,0:T(8,128)S(1)}, f32[128,128]{1,0:T(8,128)S(1)}) custom-call(f32[2048,128]{1,0:T(8,128)S(1)} %bitcast.12, f32[2048,128]{1,0:T(8,128)S(1)} %bitcast.13, f32[8,40,128]{2,1,0:T(8,128)S(1)} %bitcast.14), custom_call_target="tpu_custom_call" | custom-call | tf_op jit(solution)/shard_map/deliver/pallas_call | solution.py:237
  104.3 0.0 copy-done
  104.3 0.0 copy-done.1
  104.3 1.3 %total.1 = (f32[128,128]{1,0:T(8,128)}, f32[2048,128]{1,0:T(8,128)}, f32[512,128]{1,0:T(8,128)}) custom-call(f32[2048,128]{1,0:T(8,128)S(1)} %bitcast.11, f32[2048,128]{1,0:T(8,128)S(1)} %get-tuple-element.23.above_in, f32[2048,128]{1,0:T(8,128)S(1)} %get-tuple-element.24.below_in, f32[128,128]{1,0:T(8,128)S(1)} %get-tuple-element.25.dual_pot, ...), custom_call_target="tpu_custom_call" | custom-call | tf_op jit(solution)/shard_map/total/pallas_call | solution.py:289
Async XLA Ops:
  0.6 103.7 %copy-start = (f32[512,128]{1,0:T(8,128)S(1)}, f32[512,128]{1,0:T(8,128)}, u32[]{:S(2)}) copy-start(f32[512,128]{1,0:T(8,128)} %pot.1) | copy-start | bytes 786436
  0.6 103.7 %copy-start.1 = (f32[512,128]{1,0:T(8,128)S(1)}, f32[512,128]{1,0:T(8,128)}, u32[]{:S(2)}) copy-start(f32[512,128]{1,0:T(8,128)} %target.1) | copy-start | bytes 786436

commit v10 on v9

--- a/solution.py
+++ b/solution.py
@@ -166,7 +166,7 @@
         scratch_shapes=[
             pltpu.VMEM((3, 3, SB, BS), jnp.float32),
             pltpu.VMEM((3, SB, BS), jnp.float32),
-            pltpu.VMEM((64, BS), jnp.float32),
+            pltpu.VMEM((128, BS), jnp.float32),
             pltpu.SMEM((KC, VB), jnp.int32),
             pltpu.SMEM((N_GX * N_GY * SB,), jnp.int32),
             pltpu.VMEM((VB // BS, BS), jnp.int32),
@@ -309,7 +309,7 @@
     low_out, own_out, high_out, dual, mom, vox, mass, sems, *scratch,
 ):
     loads = [
-        pltpu.make_async_copy(vox_hbm, vox, sems.at[0]),
+        pltpu.make_async_copy(vox_hbm, vox.at[pl.ds(0, 3 * VB)], sems.at[0]),
         pltpu.make_async_copy(mass_hbm, mass, sems.at[1]),
     ]
     for load in loads:
@@ -441,7 +441,7 @@
     moments = jax.ShapeDtypeStruct((SB, 4, BS), jnp.float32)
     scratch = [
         pltpu.VMEM((POOL, 8, BS), jnp.float32),
-        pltpu.VMEM((3 * VB, BS), jnp.float32),
+        pltpu.VMEM((8 * VB, BS), jnp.float32),
         pltpu.VMEM((VB, BS), jnp.float32),
         pltpu.SemaphoreType.DMA((2,)),
     ]

time: 105 us -> 106 us (level)
  no operation moved by 1% of the time
where the time goes in v10:
time: 106 us
  Pallas kernels  105 us (99%)
    pallas_call x1, Pallas kernels, work(): pl.pallas_call(work_kernel, in_specs=[SMEM] * 2 + [HBM] * 2 + [VMEM], out...  39.4 us
    pallas_call x1, Pallas kernels, exchange(): pl.pallas_call(exchange_kernel, in_specs=[HBM] * 5, out_specs=[VMEM, SMEM...  32.1 us
    pallas_call x1, Pallas kernels, deliver(): pl.pallas_call(deliver_kernel, in_specs=[VMEM] * 3, out_specs=[VMEM] * 3,...  32.1 us

profile of v10, /device:TPU:1, one launch (start us, length us, event | category | flops | bytes accessed | tf_op | source)
XLA Modules:
  0.0 105.6 jit_solution(5765205077900432654)
XLA Ops:
  0.6 0.0 copy-start
  0.6 0.0 copy-start.1
  0.7 32.1 %exchange.1 = (bf16[1536,16,128]{2,1,0:T(8,128)(2,1)S(1)}, s32[2048]{0:T(1024)S(1)}, s32[8,256]{1,0:T(8,128)S(1)}) custom-call(f32[3,512,128]{2,1,0:T(8,128)} %bitcast.15, f32[512,128]{1,0:T(8,128)} %pot.1, s32[8,256]{1,0:T(8,128)} %bitcast.17, s32[65536]{0:T(1024)} %home_hbm.1, s32[2,128]{1,0:T(2,128)} %bitcast.18), custom_call_target="tpu_custom_call" | custom-call | tf_op jit(solution)/shard_map/exchange/pallas_call | solution.py:157
  32.8 39.4 %work.1 = (f32[512,4,128]{2,1,0:T(4,128)S(1)}, f32[512,4,128]{2,1,0:T(4,128)S(1)}, f32[512,4,128]{2,1,0:T(4,128)S(1)}, f32[320,128]{1,0:T(8,128)S(1)}) custom-call(s32[2048]{0:T(1024)S(1)} %get-tuple-element.16.pidx, s32[8,256]{1,0:T(8,128)S(1)} %get-tuple-element.17.listed, f32[768,128]{1,0:T(8,128)} %bitcast.16, f32[256,128]{1,0:T(8,128)} %mass_hbm.1, ...), custom_call_target="tpu_custom_call" | custom-call | tf_op jit(solution)/shard_map/work/pallas_call | solution.py:455
  72.2 32.1 %deliver.1 = (f32[2048,128]{1,0:T(8,128)S(1)}, f32[2048,128]{1,0:T(8,128)S(1)}, f32[128,128]{1,0:T(8,128)S(1)}) custom-call(f32[2048,128]{1,0:T(8,128)S(1)} %bitcast.12, f32[2048,128]{1,0:T(8,128)S(1)} %bitcast.13, f32[8,40,128]{2,1,0:T(8,128)S(1)} %bitcast.14), custom_call_target="tpu_custom_call" | custom-call | tf_op jit(solution)/shard_map/deliver/pallas_call | solution.py:237
  104.3 0.0 copy-done
  104.3 0.0 copy-done.1
  104.3 1.3 %total.1 = (f32[128,128]{1,0:T(8,128)}, f32[2048,128]{1,0:T(8,128)}, f32[512,128]{1,0:T(8,128)}) custom-call(f32[2048,128]{1,0:T(8,128)S(1)} %bitcast.11, f32[2048,128]{1,0:T(8,128)S(1)} %get-tuple-element.23.above_in, f32[2048,128]{1,0:T(8,128)S(1)} %get-tuple-element.24.below_in, f32[128,128]{1,0:T(8,128)S(1)} %get-tuple-element.25.dual_pot, ...), custom_call_target="tpu_custom_call" | custom-call | tf_op jit(solution)/shard_map/total/pallas_call | solution.py:289
Async XLA Ops:
  0.6 103.7 %copy-start = (f32[512,128]{1,0:T(8,128)S(1)}, f32[512,128]{1,0:T(8,128)}, u32[]{:S(2)}) copy-start(f32[512,128]{1,0:T(8,128)} %pot.1) | copy-start | bytes 786436
  0.6 103.7 %copy-start.1 = (f32[512,128]{1,0:T(8,128)S(1)}, f32[512,128]{1,0:T(8,128)}, u32[]{:S(2)}) copy-start(f32[512,128]{1,0:T(8,128)} %target.1) | copy-start | bytes 786436
